TPU v7x, 32 devices: a whole 2x2x4 slice. The times are simulated.
32 devices in a mesh: dp: 8 (over y, x, core), tensor: 4 (over z).
Axes of the slice: x: 2, y: 2, z: 4, core: 2. Of those that a mesh axis runs over, the one named last changes fastest.
Arguments:
- layer_in: bfloat16 [64, 128, 1024], P('dp', 'tensor'), may hold values from -6 to 6
- cotangent: bfloat16 [64, 128, 1024], P('dp', 'tensor'), may hold values from -8 to 8
- row_counts: int32 [16], replicated, may hold values from 1 to 8, 64 in all
- tail_tokens: int32 [16], replicated, may hold values from 1 to 128
- row_order: int32 [64], replicated, may hold values from 0 to 63, each once
- gain_one: bfloat16 [1024], P('dp'), may hold values from 0.099609375 to 1.8984375
- w_in: bfloat16 [1024, 3, 1024], P('dp', None, 'tensor'), may hold values from -0.1875 to 0.1875
- kernel: bfloat16 [3, 1024], P(None, 'dp'), may hold values from -3.5 to 3.5
- w_out: bfloat16 [1024, 1024], P('tensor', 'dp'), may hold values from -0.1875 to 0.1875
- gain_two: bfloat16 [1024], P('dp'), may hold values from 0.099609375 to 1.8984375
- w_gu: bfloat16 [1024, 2, 4608], P('dp', None, 'tensor'), may hold values from -0.1875 to 0.1875
- w_down: bfloat16 [4608, 1024], P('tensor', 'dp'), may hold values from -0.125 to 0.125
Outputs:
- layer_out: bfloat16 [64, 128, 1024], P('dp', 'tensor')
- grad_in: bfloat16 [64, 128, 1024], P('dp', 'tensor')
- grad_gain_one: float32 [1024], P('dp')
- grad_w_in: float32 [1024, 3, 1024], P('dp', None, 'tensor')
- grad_kernel: float32 [3, 1024], P(None, 'dp')
- grad_w_out: float32 [1024, 1024], P('tensor', 'dp')
- grad_gain_two: float32 [1024], P('dp')
- grad_w_gu: float32 [1024, 2, 4608], P('dp', None, 'tensor')
- grad_w_down: float32 [4608, 1024], P('tensor', 'dp')
Inputs may be any that keep to these rules, and one draw needn't show every extreme that they name: row_counts sum to 64; the longest sequence has exactly 8 rows. `row_order`: each given-order row stands in exactly one dealt slot.
All inputs are finite; a program needn't handle non-finite values.
Results may differ from a plain program's by a relative error of at most 0.025.
Values may be sent and summed in bfloat16 or wider, within the bound.
No kernel may reach another device: no remote copies, remote signals or barrier semaphores. Data moves between devices by JAX's collectives and lax.ppermute only.
A program may use at most 128 MiB of HBM per device.

v0:
```python
import functools
import jax
import jax.numpy as jnp
from jax import lax
from jax.experimental import pallas as pl
from jax.experimental.pallas import tpu as pltpu
from jax.sharding import PartitionSpec as P

EPS = 1e-05
INNER = 8
BF = jnp.bfloat16
F32 = jnp.float32
VMEM_LIMIT = 12 << 20


def hold_kernel(*refs):
    pass


def hold(value, *events):
    anywhere = pl.BlockSpec(memory_space=pl.ANY)
    return pl.pallas_call(
        hold_kernel,
        out_shape=shape(*value.shape, dtype=value.dtype),
        in_specs=[anywhere] * (1 + len(events)),
        out_specs=anywhere,
        input_output_aliases={0: 0},
        cost_estimate=pl.CostEstimate(flops=1, bytes_accessed=1, transcendentals=0),
        name="hold",
    )(value, *events)


def dp_swap(value, step, tag):
    size = lax.axis_size("dp")
    hop = step * (size // INNER)
    with jax.named_scope(f"{tag}_dp{step}"):
        return lax.ppermute(value, "dp", [(i, i ^ hop) for i in range(size)])


def z_shift(value, step, tag):
    size = lax.axis_size("tensor")
    with jax.named_scope(f"{tag}_z"):
        return lax.ppermute(value, "tensor", [(i, (i + step) % size) for i in range(size)])


def z_swap(value, step, tag):
    size = lax.axis_size("tensor")
    with jax.named_scope(f"{tag}_z{step}"):
        return lax.ppermute(value, "tensor", [(i, i ^ step) for i in range(size)])


def after(value, *events):
    return lax.optimization_barrier((value,) + events)[0]


def mm(a, b):
    return lax.dot_general(a, b, (((1,), (0,)), ((), ())), preferred_element_type=F32)


def mm_nt(a, b):
    return lax.dot_general(a, b, (((1,), (1,)), ((), ())), preferred_element_type=F32)


def mm_tn(a, b):
    return lax.dot_general(a, b, (((0,), (0,)), ((), ())), preferred_element_type=F32)


def shape(*dims, dtype=BF):
    return jax.ShapeDtypeStruct(dims, dtype)


def whole_call(kernel, name, outs, args, scalars=0, hbm=0, scratch=(), alias=None, weight=0):
    specs = [pl.BlockSpec(memory_space=pltpu.SMEM)] * scalars
    specs += [pl.BlockSpec(memory_space=pltpu.HBM)] * hbm
    specs += [pl.BlockSpec(memory_space=pltpu.VMEM)] * (len(args) - scalars - hbm)
    return pl.pallas_call(
        kernel,
        out_shape=outs,
        in_specs=specs,
        out_specs=[pl.BlockSpec(memory_space=pltpu.VMEM)] * len(outs),
        scratch_shapes=list(scratch),
        input_output_aliases=alias or {},
        compiler_params=pltpu.CompilerParams(vmem_limit_bytes=VMEM_LIMIT),
        cost_estimate=pl.CostEstimate(flops=1 + weight, bytes_accessed=1, transcendentals=0),
        name=name,
    )(*args)


def corner(value, tag):
    size = lax.axis_size("dp")
    outer = size // INNER
    pairs = []
    for i in range(size):
        hop = 2 if (i // outer) % 2 else 4
        pairs.append((i, i ^ (hop * outer)))
    with jax.named_scope(f"{tag}_corner"):
        return lax.ppermute(value, "dp", pairs)


def core_zero():
    return lax.axis_index("dp") // (lax.axis_size("dp") // INNER) % 2 == 0


def plane_gather(local, tag, *waits):
    local = after(local, *waits) if waits else local
    return dp_swap(local, 2, tag), dp_swap(local, 4, tag)


def plane_corner(over_x, over_y, tag, *waits):
    value = jnp.where(core_zero(), over_x, over_y)
    return corner(after(value, *waits) if waits else value, tag)


def plane_far(pieces, tag, *waits):
    far = hold(pieces[3], *waits) if waits else pieces[3]
    return corner(far, tag)


def plane_near(pieces, far, tag, *waits):
    far = far.astype(F32)
    first = core_zero()
    over_x = (pieces[1].astype(F32) + jnp.where(first, far, 0.0)).astype(BF)
    over_y = (pieces[2].astype(F32) + jnp.where(first, 0.0, far)).astype(BF)
    if waits:
        over_x, over_y = after(over_x, *waits), after(over_y, *waits)
    return pieces[0], dp_swap(over_x, 2, tag), dp_swap(over_y, 4, tag)


def z_send(local, tag, steps, *waits):
    local = after(local, *waits) if waits else local
    return [z_swap(local, step, tag) for step in steps]


def stack_mixer_kernel(idx_ref, small_ref, tail_ref, *refs):
    parts, out_ref = refs[:-1], refs[-1]
    z = idx_ref[1]
    rows, ch = parts[0].shape
    for s, part in enumerate(parts):
        col = pl.multiple_of(jnp.bitwise_xor(z, s) * ch, ch)
        out_ref[:rows, pl.ds(col, ch)] = part[...]
    n_small, block = small_ref.shape
    out_ref[rows : rows + n_small] = jnp.zeros((n_small, out_ref.shape[1]), BF)
    out_ref[rows : rows + n_small, :block] = small_ref[...]
    out_ref[rows + n_small :] = tail_ref[...]


def stack_mixer(index, small, tail, parts):
    rows, ch = parts[0].shape
    return whole_call(
        stack_mixer_kernel,
        "stack_mixer",
        [shape(rows + small.shape[0] + tail.shape[0], len(parts) * ch)],
        (index, small, tail, *parts),
        scalars=1,
    )[0]


def place_mixer_kernel(block, idx_ref, *refs):
    pieces, outs, sems = refs[:8], refs[8:-1], refs[-1]
    small_ref, tail_ref = outs[4], outs[5]
    me = idx_ref[0]
    n_small, n_tail = small_ref.shape[0], tail_ref.shape[0] // 8
    copies = []
    for k in range(8):
        at = pl.multiple_of(jnp.bitwise_xor(me, k) * block, block)
        for st in range(4):
            copies.append(
                pltpu.make_async_copy(
                    pieces[k].at[pl.ds(st * block, block)], outs[st].at[pl.ds(at, block)], sems.at[k, st]
                )
            )
        copies.append(
            pltpu.make_async_copy(
                pieces[k].at[pl.ds(4 * block, n_small), pl.ds(0, block)],
                small_ref.at[:, pl.ds(at, block)],
                sems.at[k, 4],
            )
        )
        copies.append(
            pltpu.make_async_copy(
                pieces[k].at[pl.ds(4 * block + n_small, n_tail)],
                tail_ref.at[pl.ds(k * n_tail, n_tail)],
                sems.at[k, 5],
            )
        )
    for copy in copies:
        copy.start()
    for copy in copies:
        copy.wait()


def place_mixer(index, pieces, block, n_small, n_tail):
    width = pieces[0].shape[1]
    return whole_call(
        functools.partial(place_mixer_kernel, block),
        "place_mixer",
        [shape(8 * block, width)] * 4 + [shape(n_small, 8 * block), shape(8 * n_tail, width)],
        (index, *pieces),
        scalars=1,
        hbm=8,
        scratch=[pltpu.SemaphoreType.DMA((8, 6))],
    )


def place_ffn_kernel(idx_ref, *refs):
    pieces, out_ref, sems = refs[:8], refs[8], refs[9]
    me = idx_ref[0]
    rows = out_ref.shape[0] // 8
    copies = []
    for k in range(8):
        at = pl.ds(pl.multiple_of(jnp.bitwise_xor(me, k) * rows, rows), rows)
        copies.append(pltpu.make_async_copy(pieces[k], out_ref.at[at], sems.at[k]))
    for copy in copies:
        copy.start()
    for copy in copies:
        copy.wait()


def place_ffn(index, pieces):
    rows, columns = pieces[0].shape
    return whole_call(
        place_ffn_kernel,
        "place_ffn",
        [shape(8 * rows, columns)],
        (index, *pieces),
        scalars=1,
        hbm=8,
        scratch=[pltpu.SemaphoreType.DMA((8,))],
    )[0]


def ffn_kernel(step, n_ref, d_ref, w_ref, *refs):
    dn_ref, part_ref, n_all_ref, d_all_ref, hid_ref, dgu_ref = refs[-6:]
    tokens = n_ref.shape[0]
    own = slice(step * tokens, (step + 1) * tokens)
    units, width = w_ref.shape[1] // 3, w_ref.shape[0]
    wide, tall = units // 3, width // 4
    n_all_ref[own] = n_ref[...]
    d_all_ref[own] = d_ref[...]

    @pl.loop(0, 3)
    def _(i):
        one = pl.multiple_of(i * wide, wide)
        two, three = pl.multiple_of(one + units, wide), pl.multiple_of(one + 2 * units, wide)
        gate = mm(n_ref[...], w_ref[:, pl.ds(one, wide)])
        up = mm(n_ref[...], w_ref[:, pl.ds(two, wide)])
        sig = jax.nn.sigmoid(gate)
        silu = gate * sig
        hid_ref[own, pl.ds(one, wide)] = (silu * up).astype(BF)
        d_hidden = mm(d_ref[...], w_ref[:, pl.ds(three, wide)])
        d_gate = d_hidden * up * (sig * (1.0 + gate * (1.0 - sig)))
        dgu_ref[own, pl.ds(one, wide)] = d_gate.astype(BF)
        dgu_ref[own, pl.ds(two, wide)] = (d_hidden * silu).astype(BF)

    @pl.loop(0, 4)
    def _(i):
        rows = pl.ds(pl.multiple_of(i * tall, tall), tall)
        dn_ref[:, rows] = mm_nt(dgu_ref[own], w_ref[rows, : 2 * units]).astype(BF)
        part_ref[:, rows] = mm_nt(hid_ref[own], w_ref[rows, 2 * units :]).astype(BF)


def ffn_whole_kernel(step, n_ref, d_ref, w_ref, *refs):
    dn_ref, part_ref, n_all_ref, d_all_ref, hid_ref, dgu_ref = refs[-6:]
    tokens = n_ref.shape[0]
    own = slice(step * tokens, (step + 1) * tokens)
    units = w_ref.shape[1] // 3
    gu, down = slice(0, 2 * units), slice(2 * units, 3 * units)
    n_all_ref[own] = n_ref[...]
    d_all_ref[own] = d_ref[...]
    both = mm(n_ref[...], w_ref[:, gu])
    gate, up = both[:, :units], both[:, units:]
    sig = jax.nn.sigmoid(gate)
    silu = gate * sig
    hidden = (silu * up).astype(BF)
    hid_ref[own] = hidden
    d_hidden = mm(d_ref[...], w_ref[:, down])
    dgu_ref[own, :units] = (d_hidden * up * (sig * (1.0 + gate * (1.0 - sig)))).astype(BF)
    dgu_ref[own, units:] = (d_hidden * silu).astype(BF)
    dn_ref[...] = mm_nt(dgu_ref[own], w_ref[:, gu]).astype(BF)
    part_ref[...] = mm_nt(hidden, w_ref[:, down]).astype(BF)


def ffn_piece(step, steps, normed, d_out, weights, kept):
    tokens, width = normed.shape
    units = weights.shape[1] // 3
    every = steps * tokens
    return whole_call(
        functools.partial(ffn_kernel if step < 2 else ffn_whole_kernel, step),
        "ffn_piece",
        [shape(tokens, width)] * 2
        + [shape(every, width), shape(every, width), shape(every, units), shape(every, 2 * units)],
        (normed, d_out, weights, *kept),
        alias={3 + i: 2 + i for i in range(len(kept))},
    )


def norm_scale(value):
    return lax.rsqrt(jnp.mean(value * value, axis=-1, keepdims=True) + EPS)


def norm_back(d_normed, value, scale, gain):
    weighted = d_normed * gain
    d_value = scale * weighted - value * (scale * scale * scale) * jnp.mean(
        weighted * value, axis=-1, keepdims=True
    )
    return d_value, jnp.sum(d_normed * value * scale, axis=0, keepdims=True)


def halo_picks(tokens, own_len, halo):
    token = lax.broadcasted_iota(jnp.int32, (tokens, halo), 0)
    slot = lax.broadcasted_iota(jnp.int32, (tokens, halo), 1)
    run, pos = token // own_len, token % own_len
    one = jnp.logical_and(pos == 0, slot == 2 * run + 1)
    two = jnp.logical_and(pos < 2, slot == 2 * run + pos)
    return one.astype(BF), two.astype(BF)


def earlier(mixed, mixed_halo, own_len):
    tokens = mixed.shape[0]
    pick_one, pick_two = halo_picks(tokens, own_len, mixed_halo.shape[0])
    pos = lax.broadcasted_iota(jnp.int32, mixed.shape, 0) % own_len
    one = jnp.where(pos == 0, mm(pick_one, mixed_halo), pltpu.roll(mixed, 1, axis=0))
    two = jnp.where(pos < 2, mm(pick_two, mixed_halo), pltpu.roll(mixed, 2, axis=0))
    return one, two


def mixer_in_kernel(
    own_len, x_ref, xh_ref, small_ref, wb_ref, wu_ref, n_ref, nh_ref, b_ref, u_ref, bh_ref, uh_ref, mix_ref, mixh_ref, conv_ref
):
    gain = small_ref[0:1].astype(F32)
    x, xh = x_ref[...].astype(F32), xh_ref[...].astype(F32)
    n_ref[...] = (x * norm_scale(x) * gain).astype(BF)
    nh_ref[...] = (xh * norm_scale(xh) * gain).astype(BF)
    b_ref[...] = mm(n_ref[...], wb_ref[...])
    u_ref[...] = mm(n_ref[...], wu_ref[...])
    bh_ref[...] = mm(nh_ref[...], wb_ref[...])
    uh_ref[...] = mm(nh_ref[...], wu_ref[...])
    mix_ref[...] = (b_ref[...] * u_ref[...]).astype(BF)
    mixh_ref[...] = (bh_ref[...] * uh_ref[...]).astype(BF)
    mixed = mix_ref[...].astype(F32)
    one, two = earlier(mixed, mixh_ref[...], own_len)
    taps = [small_ref[2 + k : 3 + k].astype(F32) for k in range(3)]
    conv_ref[...] = taps[0] * two + taps[1] * one + taps[2] * mixed


def mixer_in(own_len, x, x_halo, small, w_b, w_u):
    (tokens, width), halo, ch = x.shape, x_halo.shape[0], w_b.shape[1]
    return whole_call(
        functools.partial(mixer_in_kernel, own_len),
        "mixer_in",
        [
            shape(tokens, width),
            shape(halo, width),
            shape(tokens, ch, dtype=F32),
            shape(tokens, ch, dtype=F32),
            shape(halo, ch, dtype=F32),
            shape(halo, ch, dtype=F32),
            shape(tokens, ch),
            shape(halo, ch),
            shape(tokens, ch, dtype=F32),
        ],
        (x, x_halo, small, w_b, w_u),
    )


def mixer_out_kernel(x_ref, n_ref, conv_ref, small_ref, wc_ref, wo_ref, c_ref, gated_ref, mid_ref, n2_ref):
    c_ref[...] = mm(n_ref[...], wc_ref[...])
    gated_ref[...] = (c_ref[...] * conv_ref[...]).astype(BF)
    mid = x_ref[...].astype(F32) + mm_nt(gated_ref[...], wo_ref[...])
    mid_ref[...] = mid
    n2_ref[...] = (mid * norm_scale(mid) * small_ref[1:2].astype(F32)).astype(BF)


def mixer_out(x, n_one, conv, small, w_c, w_o):
    (tokens, width), ch = x.shape, w_c.shape[1]
    return whole_call(
        mixer_out_kernel,
        "mixer_out",
        [
            shape(tokens, ch, dtype=F32),
            shape(tokens, ch),
            shape(tokens, width, dtype=F32),
            shape(tokens, width),
        ],
        (x, n_one, conv, small, w_c, w_o),
    )


def mixer_back_kernel(own_len, n_parts, *refs):
    parts = refs[:n_parts]
    (mid_ref, dy_ref, x_ref, xh_ref, small_ref, b_ref, u_ref, c_ref, bh_ref, uh_ref, mix_ref, mixh_ref, conv_ref) = refs[
        n_parts : n_parts + 13
    ]
    wb_ref, wu_ref, wc_ref, wo_ref = refs[n_parts + 13 : n_parts + 17]
    dmix_ref, db_ref, du_ref, dc_ref, dbh_ref, duh_ref, gin_ref, dxh_ref, sg_ref = refs[n_parts + 17 :]
    gain_one, gain_two = small_ref[0:1].astype(F32), small_ref[1:2].astype(F32)
    taps = [small_ref[2 + k : 3 + k].astype(F32) for k in range(3)]
    d_n2 = parts[0][...].astype(F32)
    for part in parts[1:]:
        d_n2 = d_n2 + part[...].astype(F32)
    mid = mid_ref[...]
    d_mid, g_two = norm_back(d_n2, mid, norm_scale(mid), gain_two)
    d_mid = d_mid + dy_ref[...].astype(F32)
    dmix_ref[...] = d_mid.astype(BF)
    d_gated = mm(dmix_ref[...], wo_ref[...])
    dc_ref[...] = (d_gated * conv_ref[...]).astype(BF)
    d_conv = d_gated * c_ref[...]
    mixed = mix_ref[...].astype(F32)
    one, two = earlier(mixed, mixh_ref[...], own_len)
    tap_rows = [jnp.sum(d_conv * view, axis=0, keepdims=True) for view in (two, one, mixed)]
    tokens = mixed.shape[0]
    pos = lax.broadcasted_iota(jnp.int32, mixed.shape, 0) % own_len
    d_mixed = taps[2] * d_conv
    d_mixed = d_mixed + taps[1] * jnp.where(pos < own_len - 1, pltpu.roll(d_conv, tokens - 1, axis=0), 0.0)
    d_mixed = d_mixed + taps[0] * jnp.where(pos < own_len - 2, pltpu.roll(d_conv, tokens - 2, axis=0), 0.0)
    db_ref[...] = (d_mixed * u_ref[...]).astype(BF)
    du_ref[...] = (d_mixed * b_ref[...]).astype(BF)
    pick_one, pick_two = halo_picks(tokens, own_len, mixh_ref.shape[0])
    low = d_conv.astype(BF)
    d_halo = taps[1] * mm_tn(pick_one, low) + taps[0] * mm_tn(pick_two, low)
    dbh_ref[...] = (d_halo * uh_ref[...]).astype(BF)
    duh_ref[...] = (d_halo * bh_ref[...]).astype(BF)
    d_n1 = mm_nt(db_ref[...], wb_ref[...]) + mm_nt(du_ref[...], wu_ref[...]) + mm_nt(dc_ref[...], wc_ref[...])
    x, xh = x_ref[...].astype(F32), xh_ref[...].astype(F32)
    d_x, g_one = norm_back(d_n1, x, norm_scale(x), gain_one)
    gin_ref[...] = d_x + d_mid
    d_nh = mm_nt(dbh_ref[...], wb_ref[...]) + mm_nt(duh_ref[...], wu_ref[...])
    d_xh, g_halo = norm_back(d_nh, xh, norm_scale(xh), gain_one)
    dxh_ref[...] = d_xh.astype(BF)
    for row, value in enumerate([g_one + g_halo, g_two] + tap_rows):
        sg_ref[row : row + 1] = value
    sg_ref[5:8] = jnp.zeros((3, sg_ref.shape[1]), F32)


def mixer_back(own_len, parts, saved, weights):
    (tokens, width), ch = parts[0].shape, weights[0].shape[1]
    halo = saved[3].shape[0]
    return whole_call(
        functools.partial(mixer_back_kernel, own_len, len(parts)),
        "mixer_back",
        [shape(tokens, width)]
        + [shape(tokens, ch)] * 3
        + [shape(halo, ch)] * 2
        + [shape(tokens, width, dtype=F32), shape(halo, width), shape(8, width, dtype=F32)],
        (*parts, *saved, *weights),
        weight=60000000000,
    )


def mixer_grad_kernel(with_halo, idx_ref, *refs):
    n_in = 8 if with_halo else 4
    ins, away_ref, home_ref = refs[:n_in], refs[n_in], refs[n_in + 1]
    me = idx_ref[0]
    quad, core = me // 2, lax.rem(me, 2)
    width = away_ref.shape[2]
    rows = ins[0].shape[1] // 8

    @pl.loop(0, 4)
    def _(kq):
        chip = jnp.bitwise_xor(quad, kq) * 2
        away = pl.multiple_of((chip + 1 - core) * rows, rows)
        home = pl.multiple_of((chip + core) * rows, rows)
        for st in range(2):
            left_ref, right_ref = ins[2 * st], ins[2 * st + 1]
            left = jnp.concatenate([left_ref[:, pl.ds(away, rows)], left_ref[:, pl.ds(home, rows)]], axis=1)
            grad = mm_tn(left, right_ref[...])
            if with_halo:
                nh_ref = ins[4]
                left = jnp.concatenate([nh_ref[:, pl.ds(away, rows)], nh_ref[:, pl.ds(home, rows)]], axis=1)
                grad = grad + mm_tn(left, ins[5][:, st * width : (st + 1) * width])
            grad = grad.astype(BF)
            away_ref[kq, st * rows : (st + 1) * rows] = grad[:rows]
            home_ref[kq, st * rows : (st + 1) * rows] = grad[rows:]
        if with_halo:
            n_tail = ins[7].shape[0] // 8
            for ref, at, k in ((away_ref, away, 2 * kq + 1), (home_ref, home, 2 * kq)):
                values = ins[6][:, pl.ds(at, rows)]
                values = jnp.concatenate([values, jnp.zeros_like(values)], axis=0)
                ref[kq, 2 * rows : 2 * rows + 16] = jnp.zeros((16, width), BF)
                ref[kq, 2 * rows : 2 * rows + 16, :rows] = values.astype(BF)
                ref[kq, 2 * rows + 16 :] = ins[7][pl.ds(pl.multiple_of(k * n_tail, n_tail), n_tail)]


def mixer_grads(index, ins, rows, with_halo):
    extra = 16 + ins[7].shape[0] // 8 if with_halo else 0
    return whole_call(
        functools.partial(mixer_grad_kernel, with_halo),
        "grads_in" if with_halo else "grads_out",
        [shape(4, 2 * rows + extra, ins[1].shape[1])] * 2,
        (index, *ins),
        scalars=1,
    )


def split_kernel(rows, idx_ref, *refs):
    terms, outs = refs[:3], refs[3:]
    z = idx_ref[1]
    n_z = len(outs)
    ch = terms[0].shape[1] // n_z
    n_tail = terms[0].shape[0] - rows - 16
    ahead = jnp.bitwise_xor(z, lax.rem(z + n_z - 1, n_z))

    def total(at, col):
        return sum(term[at, col].astype(F32) for term in terms).astype(BF)

    for s, out in enumerate(outs):
        out[:rows] = total(slice(0, rows), pl.ds(pl.multiple_of(jnp.bitwise_xor(z, s) * ch, ch), ch))
        if n_tail > 0:
            out[rows : rows + 16] = total(slice(rows, rows + 16), slice(0, ch))
            for c in range(n_z):
                value = total(slice(rows + 16, rows + 16 + n_tail), slice(c * ch, (c + 1) * ch))
                at = rows + 16 + c * n_tail
                out[at : at + n_tail] = jnp.where(ahead == s, value, jnp.zeros_like(value))


def split_z(index, terms, rows, n_z):
    every, width = terms[0].shape
    extra = 16 + (every - rows - 16) * n_z if every > rows else 0
    return whole_call(
        functools.partial(split_kernel, rows),
        "split_z",
        [shape(rows + extra, width // n_z)] * n_z,
        (index, *terms),
        scalars=1,
    )


def finish_co_kernel(*refs):
    parts, (c_ref, out_ref) = refs[:-2], refs[-2:]
    block = c_ref.shape[0]
    total = sum(part[...].astype(F32) for part in parts)
    c_ref[...] = total[:block]
    out_ref[...] = total[block:].T


def finish_co(parts):
    rows, ch = parts[0].shape
    outs = [shape(rows // 2, ch, dtype=F32), shape(ch, rows // 2, dtype=F32)]
    return whole_call(finish_co_kernel, "finish_co", outs, tuple(parts))


def finish_bu_kernel(own_len, reach, *refs):
    n_z = len(refs) - 5
    parts = refs[:n_z]
    c_ref, mid_ref, w_ref, small_ref, in_ref = refs[n_z:]
    block, ch = c_ref.shape
    tokens = mid_ref.shape[0]

    def total(lo, hi):
        return sum(part[lo:hi].astype(F32) for part in parts)

    w_ref[0] = total(0, block)
    w_ref[1] = c_ref[...]
    w_ref[2] = total(block, 2 * block)
    small_ref[...] = total(2 * block, 2 * block + 16)[:8, :block]
    n_tail = tokens // own_len * reach
    token = lax.broadcasted_iota(jnp.int32, (tokens, n_tail), 0)
    slot = lax.broadcasted_iota(jnp.int32, (tokens, n_tail), 1)
    ahead = own_len - reach + slot % reach
    spread = jnp.logical_and(token // own_len == slot // reach, token % own_len == ahead).astype(BF)
    for c in range(n_z):
        lo = 2 * block + 16 + c * n_tail
        cols = slice(c * ch, (c + 1) * ch)
        back = mm(spread, total(lo, lo + n_tail).astype(BF))
        in_ref[:, cols] = (mid_ref[:, cols] + back).astype(BF)


def finish_bu(parts, grad_c, grad_mid, own_len, reach):
    block, ch = grad_c.shape
    return whole_call(
        functools.partial(finish_bu_kernel, own_len, reach),
        "finish_bu",
        [shape(3, block, ch, dtype=F32), shape(8, block, dtype=F32), shape(*grad_mid.shape)],
        (*parts, grad_c, grad_mid),
    )


def ffn_grad_kernel(first, count, idx_ref, n_ref, d_ref, hid_ref, dgu_ref, away_ref, home_ref):
    me = idx_ref[0]
    quad, core = me // 2, lax.rem(me, 2)
    rows = n_ref.shape[1] // 8
    split = dgu_ref.shape[1]

    @pl.loop(0, count)
    def _(i):
        chip = jnp.bitwise_xor(quad, first + i) * 2
        away = pl.multiple_of((chip + 1 - core) * rows, rows)
        home = pl.multiple_of((chip + core) * rows, rows)
        left = jnp.concatenate([n_ref[:, pl.ds(away, rows)], n_ref[:, pl.ds(home, rows)]], axis=1)
        grad = mm_tn(left, dgu_ref[...]).astype(BF)
        away_ref[i, :, :split] = grad[:rows]
        home_ref[i, :, :split] = grad[rows:]
        left = jnp.concatenate([d_ref[:, pl.ds(away, rows)], d_ref[:, pl.ds(home, rows)]], axis=1)
        grad = mm_tn(left, hid_ref[...]).astype(BF)
        away_ref[i, :, split:] = grad[:rows]
        home_ref[i, :, split:] = grad[rows:]


def ffn_grads(index, first, count, n_all, d_all, hid_all, dgu_all):
    rows = n_all.shape[1] // 8
    columns = hid_all.shape[1] + dgu_all.shape[1]
    return whole_call(
        functools.partial(ffn_grad_kernel, first, count),
        "ffn_grads",
        [shape(count, rows, columns)] * 2,
        (index, n_all, d_all, hid_all, dgu_all),
        scalars=1,
    )


def core_sum(away, home, count, tag):
    other = dp_swap(away, 1, tag)
    return [(home[kq].astype(F32) + other[kq].astype(F32)).astype(BF) for kq in range(count)]


def body(
    layer_in,
    cotangent,
    row_counts,
    tail_tokens,
    row_order,
    gain_one,
    w_in,
    kernel,
    w_out,
    gain_two,
    w_gu,
    w_down,
):
    row_count, own_len, width = layer_in.shape
    n_dp, n_z = lax.axis_size("dp"), lax.axis_size("tensor")
    outer = n_dp // INNER
    me, z = lax.axis_index("dp"), lax.axis_index("tensor")
    me_in = me // outer
    row_len = own_len * n_z
    channels = w_in.shape[2]
    reach = kernel.shape[0] - 1
    tokens = row_count * own_len
    block = width // INNER
    units = w_down.shape[0]
    index = jnp.stack([me_in, z]).astype(jnp.int32)

    given = lax.dynamic_slice_in_dim(row_order, me * row_count, row_count)
    starts = jnp.cumsum(row_counts) - row_counts
    ends = starts + row_counts - 1
    is_first = jnp.any(starts[None, :] == given[:, None], axis=1)
    at_end = ends[None, :] == given[:, None]
    row_valid = jnp.where(
        jnp.any(at_end, axis=1),
        jnp.sum(jnp.where(at_end, tail_tokens[None, :], 0), axis=1),
        row_len,
    )
    positions = z * own_len + jnp.arange(own_len, dtype=jnp.int32)
    valid = positions[None, :] < row_valid[:, None]

    small = jnp.concatenate([gain_one[None], gain_two[None], kernel], axis=0)
    mix_own = jnp.stack([w_in[:, 0], w_in[:, 2], w_in[:, 1], w_out.T])
    ffn_own = jnp.concatenate([w_gu[:, 0], w_gu[:, 1], w_down.T], axis=1)
    groups = [[i * outer + o for o in range(outer)] for i in range(INNER)]
    tails = layer_in[:, own_len - reach :].reshape(row_count * reach, width)
    tails = z_shift(tails, 1, "tail")
    if outer > 1:
        wide = functools.partial(lax.all_gather, axis_name="dp", tiled=True, axis_index_groups=groups)
        mix_own, small = wide(mix_own, axis=1), wide(small, axis=1)
        ffn_own, tails = wide(ffn_own, axis=0), wide(tails, axis=0)
    n_small = small.shape[0]
    small = jnp.pad(small, ((0, 16 - n_small), (0, 0)))
    mix_own = after(mix_own.reshape(4 * block, channels), ffn_own)

    mix_far, mix_near = z_send(mix_own, "mix", (2, 1))
    ffn_x, ffn_y = plane_gather(ffn_own, "ffn")
    mix_last = z_swap(mix_far, 1, "mix_on")
    d_ffn = jnp.where(valid[:, :, None], cotangent, jnp.zeros_like(cotangent)).reshape(tokens, width)
    tails = after(tails, d_ffn)
    mix_rows = stack_mixer(index, small, tails, [mix_own, mix_near, mix_far, mix_last])

    mix_rows = after(mix_rows, ffn_x, ffn_y)
    mix_x, mix_y = plane_gather(mix_rows, "mix")
    dy_far, dy_near = z_send(d_ffn, "dy", (2, 1), mix_last)
    mix_pairs = [mix_rows, dp_swap(mix_rows, 1, "mix")]
    ffn_pairs = [ffn_own, dp_swap(ffn_own, 1, "ffn")]
    ffn_pairs += [ffn_x, dp_swap(after(ffn_x, ffn_pairs[1]), 1, "ffn")]
    mix_d = plane_corner(mix_x, mix_y, "mix", dy_far, dy_near, ffn_pairs[1])
    ffn_pairs += [ffn_y, dp_swap(after(ffn_y, ffn_pairs[3]), 1, "ffn")]
    dy_set = [dy_near, dy_far, z_swap(dy_far, 1, "dy_on")]
    mix_pairs += [mix_x, dp_swap(mix_x, 1, "mix"), mix_y, dp_swap(mix_y, 1, "mix")]
    mix_pairs += [mix_d, dp_swap(after(mix_d, ffn_pairs[3], dy_set[2]), 1, "mix")]
    w_b, w_u, w_c, w_o, small_all, every = place_mixer(index, mix_pairs, block, 16, tails.shape[0])

    slots = INNER * outer * row_count
    rel = jnp.bitwise_xor(me_in, jnp.arange(INNER, dtype=jnp.int32))
    slot_rows = row_order.reshape(INNER, outer * row_count)[rel].reshape(slots)
    wanted = jnp.where(z == 0, jnp.where(is_first, -1, given - 1), given)
    picks = jnp.repeat(wanted, reach)[:, None] == jnp.repeat(slot_rows, reach)[None, :]
    picks = jnp.logical_and(
        picks, jnp.arange(row_count * reach)[:, None] % reach == jnp.arange(slots * reach)[None, :] % reach
    ).astype(BF)
    x_halo = mm(picks, every).astype(BF)
    x_own = layer_in.reshape(tokens, width)
    n_one, n_halo, b_own, u_own, b_halo, u_halo, mixed, mixed_halo, conv = mixer_in(
        own_len, x_own, x_halo, small_all, w_b, w_u
    )
    c_own, gated, middle, n_two = mixer_out(x_own, n_one, conv, small_all, w_c, w_o)

    ffn_d = plane_corner(ffn_x, ffn_y, "ffn", mix_d)
    n_two_far, n_two_near = z_send(n_two, "n2", (2, 1))
    n_two_set = [n_two, n_two_near, n_two_far]
    ffn_pairs += [ffn_d, dp_swap(after(ffn_d, n_two), 1, "ffn")]
    w_ffn = place_ffn(index, ffn_pairs)
    d_ffn_set = [d_ffn] + dy_set
    d_parts, out_parts, kept = [], [], ()
    for s in range(n_z):
        d_part, out_part, *kept = ffn_piece(s, n_z, n_two_set[s], d_ffn_set[s], w_ffn, kept)
        d_parts.append(d_part)
        out_parts.append(out_part)
        if s == 0:
            n_two_set.append(z_swap(after(n_two_far, d_part), 1, "n2_on"))
    d_on = z_swap(d_parts[3], 1, "dn_on")
    away, home = ffn_grads(index, 0, 4, *kept)
    d_on = after(d_on, away).astype(F32) + d_parts[2].astype(F32)
    d_near = z_swap(after(d_parts[1], n_two_set[3]), 1, "dn")
    d_parts = [d_parts[0], d_near, z_swap(d_on.astype(BF), 2, "dn")]

    ffn_pieces = core_sum(away, home, 4, "gf")
    ffn_across = plane_far(ffn_pieces, "gf")
    out_on = z_swap(after(out_parts[3], d_near), 1, "out_on")
    out_first = z_swap(after(out_parts[1], d_near), 1, "out")
    d_mix, d_b, d_u, d_c, d_b_halo, d_u_halo, grad_mid, d_x_halo, small_grads = mixer_back(
        own_len,
        d_parts,
        (middle, d_ffn, x_own, x_halo, small_all, b_own, u_own, c_own, b_halo, u_halo, mixed, mixed_halo, conv),
        (w_b, w_u, w_c, w_o),
    )

    co_away, co_home = mixer_grads(index, (after(n_one, ffn_pieces[3]), d_c, d_mix, gated), block, False)
    d_bu_halo = jnp.concatenate([d_b_halo, d_u_halo], axis=1)
    spread = mm_tn(picks, d_x_halo).astype(BF)
    bu_away, bu_home = mixer_grads(
        index, (after(n_one, co_away), d_b, n_one, d_u, n_halo, d_bu_halo, small_grads, spread), block, True
    )
    co_pieces = core_sum(after(co_away, out_on), co_home, 4, "gco")
    out_second = (out_parts[2].astype(F32) + out_on.astype(F32)).astype(BF)
    out_second = z_swap(out_second, 2, "out")
    co_across = plane_far(co_pieces, "gco")
    co_terms = plane_near(co_pieces, co_across, "gco")
    bu_pieces = core_sum(after(bu_away, co_pieces[0]), bu_home, 4, "gbu")
    bu_across = plane_far(bu_pieces, "gbu")
    bu_terms = plane_near(bu_pieces, bu_across, "gbu")
    ffn_terms = plane_near(ffn_pieces, ffn_across, "gf", bu_across)
    layer_out = middle + out_parts[0].astype(F32) + out_first.astype(F32) + out_second.astype(F32)
    layer_out = layer_out.astype(BF).reshape(row_count, own_len, width)

    def z_parts(terms, tag, *waits):
        first = after(terms[0], *waits) if waits else terms[0]
        parts = split_z(index, (first, *terms[1:]), 2 * block, n_z)
        return [parts[0]] + [z_swap(parts[s], s, tag) for s in range(1, n_z)]

    co_parts = z_parts(co_terms, "gco", out_first, out_second)
    ffn_total = sum(term.astype(F32) for term in ffn_terms)
    if outer > 1:
        narrow = functools.partial(
            lax.psum_scatter, axis_name="dp", tiled=True, axis_index_groups=groups
        )
        ffn_total = narrow(ffn_total, scatter_dimension=0)
    grad_w_gu = jnp.stack([ffn_total[:, :units], ffn_total[:, units : 2 * units]], axis=1)
    grad_w_down = ffn_total[:, 2 * units :].T
    bu_parts = z_parts(bu_terms, "gbu", co_parts[0])
    if outer > 1:
        bu_total = sum(part.astype(F32) for part in bu_parts)
        grad_co = sum(part.astype(F32) for part in co_parts).reshape(2, block, channels)
        grad_co = narrow(grad_co, scatter_dimension=1)
        grad_bu = narrow(bu_total[: 2 * block].reshape(2, block, channels), scatter_dimension=1)
        grad_small = narrow(bu_total[2 * block : 2 * block + n_small, :block], scatter_dimension=1)
        returned = bu_total[2 * block + 16 :].reshape(n_z, -1, channels)
        returned = narrow(jnp.moveaxis(returned, 0, 1).reshape(-1, width), scatter_dimension=0)
        grad_w_in = jnp.stack([grad_bu[0], grad_co[0], grad_bu[1]])
        grad_w_out = grad_co[1].T
        grad_in = grad_mid.reshape(row_count, own_len, width)
        grad_in = grad_in + jnp.pad(
            returned.reshape(row_count, reach, width), ((0, 0), (own_len - reach, 0), (0, 0))
        )
        grad_in = grad_in.astype(BF)
    else:
        grad_c, grad_w_out = finish_co(co_parts)
        grad_w_in, grad_small, grad_in = finish_bu(bu_parts, grad_c, grad_mid, own_len, reach)
        grad_in = grad_in.reshape(row_count, own_len, width)
    return (
        layer_out,
        grad_in,
        grad_small[0],
        jnp.swapaxes(grad_w_in, 0, 1),
        grad_small[2:n_small],
        grad_w_out,
        grad_small[1],
        grad_w_gu,
        grad_w_down,
    )


def solution(mesh):
    in_specs = (
        P("dp", "tensor", None),
        P("dp", "tensor", None),
        P(),
        P(),
        P(),
        P("dp"),
        P("dp", None, "tensor"),
        P(None, "dp"),
        P("tensor", "dp"),
        P("dp"),
        P("dp", None, "tensor"),
        P("tensor", "dp"),
    )
    out_specs = (
        P("dp", "tensor", None),
        P("dp", "tensor", None),
        P("dp"),
        P("dp", None, "tensor"),
        P(None, "dp"),
        P("tensor", "dp"),
        P("dp"),
        P("dp", None, "tensor"),
        P("tensor", "dp"),
    )
    return jax.shard_map(body, mesh=mesh, in_specs=in_specs, out_specs=out_specs, check_vma=False)
```

profile of v0, /device:TPU:0, one launch (start us, length us, event | category | flops | bytes accessed | tf_op | source)
XLA Modules:
  0.0 272.9 jit_solution(7252610233495776308)
XLA Ops:
  0.7 1.0 fusion.41
  4.4 4.1 %collective-permute-start.2 = (bf16[512,256]{1,0:T(8,128)(2,1)S(1)}, bf16[512,256]{1,0:T(8,128)(2,1)S(1)}, u32[]{:S(2)}, u32[]{:S(2)}) collective-permute-start(bf16[512,256]{1,0:T(8,128)(2,1)S(1)} %bitcast.84), channel_id=1, source_target_pairs={{0,2},{1,3},{2,0},{3,1},{4,6},{5,7},{6,4},{7,5},{8,10},{9,11},{10,... | collective-permute-start | bytes 786440 | tf_op jit(solution)/shard_map/mix_z2/ppermute | solution.py:49
  8.5 1.6 collective-permute-start.1
  10.1 1.5 collective-permute-start.5
  11.6 1.5 collective-permute-start.4
  15.4 5.1 %collective-permute-done.2.refs_2_ = bf16[512,256]{1,0:T(8,128)(2,1)S(1)} collective-permute-done((bf16[512,256]{1,0:T(8,128)(2,1)S(1)}, bf16[512,256]{1,0:T(8,128)(2,1)S(1)}, u32[]{:S(2)}, u32[]{:S(2)}) %collective-permute-start.2) | collective-permute-done | bytes 262176 | tf_op jit(solution)/shard_map/mix_z2/ppermute | solution.py:49
  22.9 5.0 %collective-permute-done.3.refs_3_ = bf16[512,256]{1,0:T(8,128)(2,1)S(1)} collective-permute-done((bf16[512,256]{1,0:T(8,128)(2,1)S(1)}, bf16[512,256]{1,0:T(8,128)(2,1)S(1)}, u32[]{:S(2)}, u32[]{:S(2)}) %collective-permute-start.3) | collective-permute-done | bytes 262176 | tf_op jit(solution)/shard_map/mix_on_z1/ppermute | solution.py:49
  29.6 1.3 collective-permute-done.5.refs_4_
  30.9 1.0 copy-done.2
  32.2 1.2 collective-permute-start.9
  33.4 1.5 collective-permute-start.7
  35.4 3.1 %collective-permute-start.11 = (bf16[256,1024]{1,0:T(8,128)(2,1)}, bf16[256,1024]{1,0:T(8,128)(2,1)}, u32[]{:S(2)}, u32[]{:S(2)}) collective-permute-start(bf16[256,1024]{1,0:T(8,128)(2,1)} %bitcast.7.d_ref.refs_4_), channel_id=1, source_target_pairs={{0,2},{1,3},{2,0},{3,1},{4,6},{5,7},{6,4},{7,5},{8,10},{9,11},{10,... | collective-permute-start | bytes 1572872 | tf_op jit(solution)/shard_map/dy_z2/ppermute | solution.py:49
  38.4 18.5 %collective-permute-done.9.refs_4_ = bf16[544,1024]{1,0:T(8,128)(2,1)S(1)} collective-permute-done((bf16[544,1024]{1,0:T(8,128)(2,1)S(1)}, bf16[544,1024]{1,0:T(8,128)(2,1)S(1)}, u32[]{:S(2)}, u32[]{:S(2)}) %collective-permute-start.9) | collective-permute-done | bytes 1114144 | tf_op jit(solution)/shard_map/mix_dp4/ppermute | solution.py:37
  56.9 1.2 collective-permute-done.7.refs_2_
  58.3 2.3 collective-permute-done.12.d_ref
  60.6 1.8 collective-permute-done.11.d_ref
  63.7 13.7 %collective-permute-done.16.d_ref = bf16[256,1024]{1,0:T(8,128)(2,1)S(1)} collective-permute-done((bf16[256,1024]{1,0:T(8,128)(2,1)}, bf16[256,1024]{1,0:T(8,128)(2,1)S(1)}, u32[]{:S(2)}, u32[]{:S(2)}) %collective-permute-start.16) | collective-permute-done | bytes 524320 | tf_op jit(solution)/shard_map/dy_on_z1/ppermute | solution.py:49
  79.7 2.2 broadcast_select_fusion.1
  81.9 1.5 collective-permute-start.19
  84.6 3.7 %place_mixer.1 = (bf16[1024,1024]{1,0:T(8,128)(2,1)S(1)}, bf16[1024,1024]{1,0:T(8,128)(2,1)S(1)}, bf16[1024,1024]{1,0:T(8,128)(2,1)S(1)}, bf16[1024,1024]{1,0:T(...) custom-call(s32[2]{0:T(128)S(1)} %pad_add_fusion.idx_ref, ...), custom_call_target="tpu_custom_call" | custom-call | flops 1 | bytes 1 | tf_op jit(solution)/shard_map/place_mixer/pallas_call | solution.py:76
  88.5 2.4 mixer_in.1
  91.0 1.4 mixer_out.1
  92.4 2.8 %collective-permute-done.19.refs_6_ = bf16[128,3456]{1,0:T(8,128)(2,1)} collective-permute-done((bf16[128,3456]{1,0:T(8,128)(2,1)}, bf16[128,3456]{1,0:T(8,128)(2,1)}, u32[]{:S(2)}, u32[]{:S(2)}) %collective-permute-start.19) | collective-permute-done | bytes 884768 | tf_op jit(solution)/shard_map/ffn_corner/ppermute | solution.py:97
  95.2 1.1 collective-permute-start.22
  96.4 1.7 collective-permute-start.21
  98.1 2.7 place_ffn.1.w_ref
  100.8 7.0 %ffn_piece.4 = (bf16[256,1024]{1,0:T(8,128)(2,1)S(1)}, bf16[256,1024]{1,0:T(8,128)(2,1)S(1)}, bf16[1024,1024]{1,0:T(8,128)(2,1)S(1)}, bf16[1024,1024]{1,0:T(8,12...) custom-call(bf16[256,1024]{1,0:T(8,128)(2,1)S(1)} %get-tuple-element.119.n_ref, ...), custom_call_target="tpu_custom_call" | custom-call | flops 1 | bytes 1 | tf_op jit(solution)/shard_map/ffn_piece/pallas_call | solution.py:76
  107.8 13.8 %collective-permute-done.22.n_ref = bf16[256,1024]{1,0:T(8,128)(2,1)S(1)} collective-permute-done((bf16[256,1024]{1,0:T(8,128)(2,1)S(1)}, bf16[256,1024]{1,0:T(8,128)(2,1)S(1)}, u32[]{:S(2)}, u32[]{:S(2)}) %collective-permute-start.22) | collective-permute-done | bytes 524320 | tf_op jit(solution)/shard_map/n2_z2/ppermute | solution.py:49
  121.7 7.1 %ffn_piece.5 = (bf16[256,1024]{1,0:T(8,128)(2,1)S(1)}, bf16[256,1024]{1,0:T(8,128)(2,1)S(1)}, bf16[1024,1024]{1,0:T(8,128)(2,1)S(1)}, bf16[1024,1024]{1,0:T(8,12...) custom-call(bf16[256,1024]{1,0:T(8,128)(2,1)S(1)} %collective-permut, ...), custom_call_target="tpu_custom_call", output_to_operand_aliasing={{2}: (3, {}), {3}: (4, {}), {4}: (5, {}), {5}: (6, {})} | custom-call | flops 1 | bytes 1 | tf_op jit(solution)/shard_map/ffn_piece/pallas_call | solution.py:76
  128.8 5.5 %ffn_piece.6 = (bf16[256,1024]{1,0:T(8,128)(2,1)S(1)}, bf16[256,1024]{1,0:T(8,128)(2,1)S(1)}, bf16[1024,1024]{1,0:T(8,128)(2,1)S(1)}, bf16[1024,1024]{1,0:T(8,12...) custom-call(bf16[256,1024]{1,0:T(8,128)(2,1)S(1)} %collective-permut, ...), custom_call_target="tpu_custom_call", output_to_operand_aliasing={{2}: (3, {}), {3}: (4, {}), {4}: (5, {}), {5}: (6, {})} | custom-call | flops 1 | bytes 1 | tf_op jit(solution)/shard_map/ffn_piece/pallas_call | solution.py:76
  134.3 1.1 collective-permute-done.23.n_ref
  135.4 4.4 %ffn_piece.7 = (bf16[256,1024]{1,0:T(8,128)(2,1)S(1)}, bf16[256,1024]{1,0:T(8,128)(2,1)S(1)}, bf16[1024,1024]{1,0:T(8,128)(2,1)S(1)}, bf16[1024,1024]{1,0:T(8,12...) custom-call(bf16[256,1024]{1,0:T(8,128)(2,1)S(1)} %collective-permut, ...), custom_call_target="tpu_custom_call", output_to_operand_aliasing={{2}: (3, {}), {3}: (4, {}), {4}: (5, {}), {5}: (6, {})} | custom-call | flops 1 | bytes 1 | tf_op jit(solution)/shard_map/ffn_piece/pallas_call | solution.py:76
  140.6 1.2 collective-permute-start.24
  141.8 9.4 %ffn_grads.1 = (bf16[4,128,3456]{2,1,0:T(8,128)(2,1)S(1)}, bf16[4,128,3456]{2,1,0:T(8,128)(2,1)S(1)}) custom-call(s32[2]{0:T(128)S(1)} %pad_add_fusion.idx_ref, bf16[1024,1024]{1,0:T(8,128)(2,1)S(1)} %get-tuple-element.145.n_ref, bf16[1024,1024]{1,0:T(8,128)(2,1)S(1)} %get-tuple-element.146.d_ref, bf16[1024,1152]{1,0:T(8,128)(2,1)S(1)} %get-tuple-element.147.hid_ref, ...), custom_call_target="tpu_custom_call" | custom-call | flops 1 | bytes 1 | tf_op jit(solution)/shard_map/ffn_grads/pallas_call | solution.py:76
  151.2 3.4 %collective-permute-done.29 = bf16[256,1024]{1,0:T(8,128)(2,1)S(1)} collective-permute-done((bf16[256,1024]{1,0:T(8,128)(2,1)S(1)}, bf16[256,1024]{1,0:T(8,128)(2,1)S(1)}, u32[]{:S(2)}, u32[]{:S(2)}) %collective-permute-start.29) | collective-permute-done | bytes 524320 | tf_op jit(solution)/shard_map/dn_on_z1/ppermute | solution.py:49
  154.8 1.6 collective-permute-start.30
  156.4 18.3 %collective-permute-done.24.refs_1_ = bf16[256,1024]{1,0:T(8,128)(2,1)S(1)} collective-permute-done((bf16[256,1024]{1,0:T(8,128)(2,1)S(1)}, bf16[256,1024]{1,0:T(8,128)(2,1)S(1)}, u32[]{:S(2)}, u32[]{:S(2)}) %collective-permute-start.24) | collective-permute-done | bytes 524320 | tf_op jit(solution)/shard_map/dn_z1/ppermute | solution.py:49
  174.7 2.3 collective-permute-done.30.refs_2_
  177.0 6.6 %mixer_back.1 = (bf16[256,1024]{1,0:T(8,128)(2,1)S(1)}, bf16[256,1024]{1,0:T(8,128)(2,1)S(1)}, bf16[256,1024]{1,0:T(8,128)(2,1)S(1)}, bf16[256,1024]{1,0:T(8,128...) custom-call(bf16[256,1024]{1,0:T(8,128)(2,1)S(1)} %get-tuple-element, ...), custom_call_target="tpu_custom_call" | custom-call | flops 60000002048 | bytes 1 | tf_op jit(solution)/shard_map/mixer_back/pallas_call | solution.py:76
  183.9 2.5 grads_out.1
  186.3 1.1 collective-permute-done.26
  187.8 3.8 %grads_in.1 = (bf16[4,288,1024]{2,1,0:T(8,128)(2,1)S(1)}, bf16[4,288,1024]{2,1,0:T(8,128)(2,1)S(1)}) custom-call(s32[2]{0:T(128)S(1)} %pad_add_fusion.idx_ref, bf16[256,1024]{1,0:T(8,128)(2,1)S(1)} %get-tuple-element.166.n_ref.refs_0_.refs_2_, bf16[256,1024]{1,0:T(8,128)(2,1)S(1)} %get-tuple-element.167.refs_1_, ...), custom_call_target="tpu_custom_call" | custom-call | flops 1 | bytes 1 | tf_op jit(solution)/shard_map/grads_in/pallas_call | solution.py:76
  192.5 1.5 collective-permute-start.33
  194.0 2.6 collective-permute-done.32
  197.1 1.6 collective-permute-start.36
  200.1 2.3 collective-permute-start.27
  203.0 1.6 collective-permute-start.35
  204.6 6.5 %collective-permute-done.36 = bf16[288,1024]{1,0:T(8,128)(2,1)S(1)} collective-permute-done((bf16[288,1024]{1,0:T(8,128)(2,1)S(1)}, bf16[288,1024]{1,0:T(8,128)(2,1)S(1)}, u32[]{:S(2)}, u32[]{:S(2)}) %collective-permute-start.36) | collective-permute-done | bytes 589856 | tf_op jit(solution)/shard_map/gbu_corner/ppermute | solution.py:97
  212.3 11.1 %collective-permute-done.25 = bf16[256,1024]{1,0:T(8,128)(2,1)S(1)} collective-permute-done((bf16[256,1024]{1,0:T(8,128)(2,1)S(1)}, bf16[256,1024]{1,0:T(8,128)(2,1)S(1)}, u32[]{:S(2)}, u32[]{:S(2)}) %collective-permute-start.25) | collective-permute-done | bytes 524320 | tf_op jit(solution)/shard_map/out_z1/ppermute | solution.py:49
  223.4 1.5 collective-permute-start.38
  226.1 1.6 collective-permute-start.46
  227.7 4.8 %collective-permute-done.35.refs_2_ = bf16[256,1024]{1,0:T(8,128)(2,1)S(1)} collective-permute-done((bf16[256,1024]{1,0:T(8,128)(2,1)S(1)}, bf16[256,1024]{1,0:T(8,128)(2,1)S(1)}, u32[]{:S(2)}, u32[]{:S(2)}) %collective-permute-start.35) | collective-permute-done | bytes 524320 | tf_op jit(solution)/shard_map/gco_dp4/ppermute | solution.py:37
  232.5 1.5 collective-permute-start.47
  234.8 1.9 collective-permute-start.42
  236.7 8.4 %collective-permute-done.38.refs_2_ = bf16[288,1024]{1,0:T(8,128)(2,1)S(1)} collective-permute-done((bf16[288,1024]{1,0:T(8,128)(2,1)S(1)}, bf16[288,1024]{1,0:T(8,128)(2,1)S(1)}, u32[]{:S(2)}, u32[]{:S(2)}) %collective-permute-start.38) | collective-permute-done | bytes 589856 | tf_op jit(solution)/shard_map/gbu_dp4/ppermute | solution.py:37
  245.2 2.7 collective-permute-start.43
  247.8 1.5 collective-permute-start.44
  250.3 7.2 %collective-permute-done.43.refs_2_ = bf16[256,256]{1,0:T(8,128)(2,1)S(1)} collective-permute-done((bf16[256,256]{1,0:T(8,128)(2,1)S(1)}, bf16[256,256]{1,0:T(8,128)(2,1)S(1)}, u32[]{:S(2)}, u32[]{:S(2)}) %collective-permute-start.43) | collective-permute-done | bytes 131104 | tf_op jit(solution)/shard_map/gco_z2/ppermute | solution.py:49
  257.5 2.4 collective-permute-start.41
  259.9 1.1 add_convert_fusion.13
  261.8 5.2 %collective-permute-done.40.refs_2_ = bf16[336,256]{1,0:T(8,128)(2,1)S(1)} collective-permute-done((bf16[336,256]{1,0:T(8,128)(2,1)S(1)}, bf16[336,256]{1,0:T(8,128)(2,1)S(1)}, u32[]{:S(2)}, u32[]{:S(2)}) %collective-permute-start.40) | collective-permute-done | bytes 172064 | tf_op jit(solution)/shard_map/gbu_z2/ppermute | solution.py:49
  267.0 1.2 finish_bu.1
  269.9 1.1 copy.62
  271.0 1.9 copy.61
  (148 shorter events, 26.6 us)
Async XLA Ops:
  0.6 2.4 copy-start.14
  0.7 2.6 copy-start.12
  4.1 10.4 %copy-start.15 = (s32[16]{0:T(128)S(1)}, s32[16]{0:T(128)}, u32[]{:S(2)}) copy-start(s32[16]{0:T(128)} %param.14) | copy-start | bytes 196
  4.1 10.7 %copy-start.16 = (s32[64]{0:T(128)S(1)}, s32[64]{0:T(128)}, u32[]{:S(2)}) copy-start(s32[64]{0:T(128)} %param.16) | copy-start | bytes 772
  4.1 10.8 %copy-start.20 = (s32[16]{0:T(128)S(1)}, s32[16]{0:T(128)}, u32[]{:S(2)}) copy-start(s32[16]{0:T(128)} %param.15) | copy-start | bytes 196
  4.2 17.0 %copy-start.13 = (bf16[8,32,1024]{2,1,0:T(8,128)(2,1)S(1)}, bf16[8,32,1024]{2,1,0:T(8,128)(2,1)}, u32[]{:S(2)}) copy-start(bf16[8,32,1024]{2,1,0:T(8,128)(2,1)} %param.13) | copy-start | bytes 1572868
  4.2 17.9 %copy-start.17 = (bf16[3,128]{1,0:T(4,128)(2,1)S(1)}, bf16[3,128]{1,0:T(4,128)(2,1)}, u32[]{:S(2)}) copy-start(bf16[3,128]{1,0:T(4,128)(2,1)} %param.19) | copy-start | bytes 2308
  4.3 17.9 %copy-start.18 = (bf16[128]{0:T(256)(128)(2,1)S(1)}, bf16[128]{0:T(256)(128)(2,1)}, u32[]{:S(2)}) copy-start(bf16[128]{0:T(256)(128)(2,1)} %param.21) | copy-start | bytes 772
  4.3 17.9 %copy-start.19 = (bf16[128]{0:T(256)(128)(2,1)S(1)}, bf16[128]{0:T(256)(128)(2,1)}, u32[]{:S(2)}) copy-start(bf16[128]{0:T(256)(128)(2,1)} %param.17) | copy-start | bytes 772
  4.3 26.6 %copy-start = (bf16[128,3456]{1,0:T(8,128)(2,1)}, bf16[128,3456]{1,0:T(8,128)(2,1)S(1)}, u32[]{:S(2)}) copy-start(bf16[128,3456]{1,0:T(8,128)(2,1)S(1)} %pad_maximum_fusion.1.refs_0_) | copy-start | bytes 2654212
  4.4 16.2 %collective-permute-start.2 = (bf16[512,256]{1,0:T(8,128)(2,1)S(1)}, bf16[512,256]{1,0:T(8,128)(2,1)S(1)}, u32[]{:S(2)}, u32[]{:S(2)}) collective-permute-start(bf16[512,256]{1,0:T(8,128)(2,1)S(1)} %bitcast.84), channel_id=1, source_target_pairs={{0,2},{1,3},{2,0},{3,1},{4,6},{5,7},{6,4},{7,5},{8,10},{9,11},{10,... | collective-permute-start | bytes 786440 | tf_op jit(solution)/shard_map/mix_z2/ppermute | solution.py:49
  8.5 13.7 %collective-permute-start.1 = (bf16[512,256]{1,0:T(8,128)(2,1)S(1)}, bf16[512,256]{1,0:T(8,128)(2,1)S(1)}, u32[]{:S(2)}, u32[]{:S(2)}) collective-permute-start(bf16[512,256]{1,0:T(8,128)(2,1)S(1)} %bitcast.85), channel_id=1, source_target_pairs={{0,1},{1,0},{2,3},{3,2},{4,5},{5,4},{6,7},{7,6},{8,9},{9,8},{10,11... | collective-permute-start | bytes 786440 | tf_op jit(solution)/shard_map/mix_z1/ppermute | solution.py:49
  10.1 20.8 %collective-permute-start.5 = (bf16[128,3456]{1,0:T(8,128)(2,1)S(1)}, bf16[128,3456]{1,0:T(8,128)(2,1)S(1)}, u32[]{:S(2)}, u32[]{:S(2)}) collective-permute-start(bf16[128,3456]{1,0:T(8,128)(2,1)S(1)} %pad_maximum_fusion.1.refs_0_), channel_id=1, source_target_pairs={{0,16},{4,20},{8,24},{12,28},{16,0},{20,4},{24,8},{28,12},{1,17},{... | collective-permute-start | bytes 2654216 | tf_op jit(solution)/shard_map/ffn_dp4/ppermute | solution.py:37
  11.6 20.7 %collective-permute-start.4 = (bf16[128,3456]{1,0:T(8,128)(2,1)S(1)}, bf16[128,3456]{1,0:T(8,128)(2,1)}, u32[]{:S(2)}, u32[]{:S(2)}) collective-permute-start(bf16[128,3456]{1,0:T(8,128)(2,1)S(1)} %pad_maximum_fusion.1.refs_0_), channel_id=1, source_target_pairs={{0,8},{4,12},{8,0},{12,4},{16,24},{20,28},{24,16},{28,20},{1,9},{5... | collective-permute-start | bytes 2654216 | tf_op jit(solution)/shard_map/ffn_dp2/ppermute | solution.py:37
  14.0 8.2 %collective-permute-start = (bf16[16,1024]{1,0:T(8,128)(2,1)S(1)}, bf16[16,1024]{1,0:T(8,128)(2,1)S(1)}, u32[]{:S(2)}, u32[]{:S(2)}) collective-permute-start(bf16[16,1024]{1,0:T(8,128)(2,1)S(1)} %reshape.217), channel_id=1, source_target_pairs={{0,1},{1,2},{2,3},{3,0},{4,5},{5,6},{6,7},{7,4},{8,9},{9,10},{10,1... | collective-permute-start | bytes 98312 | tf_op jit(solution)/shard_map/tail_z/ppermute | solution.py:43
  20.5 7.4 %collective-permute-start.3 = (bf16[512,256]{1,0:T(8,128)(2,1)S(1)}, bf16[512,256]{1,0:T(8,128)(2,1)S(1)}, u32[]{:S(2)}, u32[]{:S(2)}) collective-permute-start(bf16[512,256]{1,0:T(8,128)(2,1)S(1)} %collective-permute-done.2.refs_2_), channel_id=1, source_target_pairs={{0,1},{1,0},{2,3},{3,2},{4,5},{5,4},{6,7},{7,6},{8,9},{9,8},{10,11... | collective-permute-start | bytes 786440 | tf_op jit(solution)/shard_map/mix_on_z1/ppermute | solution.py:49
  32.2 24.7 %collective-permute-start.9 = (bf16[544,1024]{1,0:T(8,128)(2,1)S(1)}, bf16[544,1024]{1,0:T(8,128)(2,1)S(1)}, u32[]{:S(2)}, u32[]{:S(2)}) collective-permute-start(bf16[544,1024]{1,0:T(8,128)(2,1)S(1)} %stack_mixer.1.refs_0_), channel_id=1, source_target_pairs={{0,16},{4,20},{8,24},{12,28},{16,0},{20,4},{24,8},{28,12},{1,17},{... | collective-permute-start | bytes 3342344 | tf_op jit(solution)/shard_map/mix_dp4/ppermute | solution.py:37
  33.4 24.7 %collective-permute-start.7 = (bf16[544,1024]{1,0:T(8,128)(2,1)S(1)}, bf16[544,1024]{1,0:T(8,128)(2,1)S(1)}, u32[]{:S(2)}, u32[]{:S(2)}) collective-permute-start(bf16[544,1024]{1,0:T(8,128)(2,1)S(1)} %stack_mixer.1.refs_0_), channel_id=1, source_target_pairs={{0,8},{4,12},{8,0},{12,4},{16,24},{20,28},{24,16},{28,20},{1,9},{5... | collective-permute-start | bytes 3342344 | tf_op jit(solution)/shard_map/mix_dp2/ppermute | solution.py:37
  34.9 23.3 %collective-permute-start.13 = (bf16[128,3456]{1,0:T(8,128)(2,1)}, bf16[128,3456]{1,0:T(8,128)(2,1)}, u32[]{:S(2)}, u32[]{:S(2)}) collective-permute-start(bf16[128,3456]{1,0:T(8,128)(2,1)} %copy-done), channel_id=1, source_target_pairs={{0,4},{4,0},{8,12},{12,8},{16,20},{20,16},{24,28},{28,24},{1,5},{5... | collective-permute-start | bytes 2654216 | tf_op jit(solution)/shard_map/ffn_dp1/ppermute | solution.py:37
  34.9 25.6 %collective-permute-start.12 = (bf16[256,1024]{1,0:T(8,128)(2,1)}, bf16[256,1024]{1,0:T(8,128)(2,1)}, u32[]{:S(2)}, u32[]{:S(2)}) collective-permute-start(bf16[256,1024]{1,0:T(8,128)(2,1)} %bitcast.7.d_ref.refs_4_), channel_id=1, source_target_pairs={{0,1},{1,0},{2,3},{3,2},{4,5},{5,4},{6,7},{7,6},{8,9},{9,8},{10,11... | collective-permute-start | bytes 1572872 | tf_op jit(solution)/shard_map/dy_z1/ppermute | solution.py:49
  35.4 27.0 %collective-permute-start.11 = (bf16[256,1024]{1,0:T(8,128)(2,1)}, bf16[256,1024]{1,0:T(8,128)(2,1)}, u32[]{:S(2)}, u32[]{:S(2)}) collective-permute-start(bf16[256,1024]{1,0:T(8,128)(2,1)} %bitcast.7.d_ref.refs_4_), channel_id=1, source_target_pairs={{0,2},{1,3},{2,0},{3,1},{4,6},{5,7},{6,4},{7,5},{8,10},{9,11},{10,... | collective-permute-start | bytes 1572872 | tf_op jit(solution)/shard_map/dy_z2/ppermute | solution.py:49
  38.4 41.2 %copy-start.3 = (bf16[128,3456]{1,0:T(8,128)(2,1)S(1)}, bf16[128,3456]{1,0:T(8,128)(2,1)}, u32[]{:S(2)}) copy-start(bf16[128,3456]{1,0:T(8,128)(2,1)} %copy-done.2) | copy-start | bytes 2654212
  62.4 16.8 %collective-permute-start.14 = (bf16[544,1024]{1,0:T(8,128)(2,1)S(1)}, bf16[544,1024]{1,0:T(8,128)(2,1)}, u32[]{:S(2)}, u32[]{:S(2)}) collective-permute-start(bf16[544,1024]{1,0:T(8,128)(2,1)S(1)} %broadcast_select_fusion), channel_id=1, source_target_pairs={{0,16},{4,12},{8,24},{12,4},{16,0},{20,28},{24,8},{28,20},{1,17},{... | collective-permute-start | bytes 3342344 | tf_op jit(solution)/shard_map/mix_corner/ppermute | solution.py:97
  62.9 15.3 %collective-permute-start.15 = (bf16[128,3456]{1,0:T(8,128)(2,1)}, bf16[128,3456]{1,0:T(8,128)(2,1)S(1)}, u32[]{:S(2)}, u32[]{:S(2)}) collective-permute-start(bf16[128,3456]{1,0:T(8,128)(2,1)} %collective-permute-done.4.refs_2_), channel_id=1, source_target_pairs={{0,4},{4,0},{8,12},{12,8},{16,20},{20,16},{24,28},{28,24},{1,5},{5... | collective-permute-start | bytes 2654216 | tf_op jit(solution)/shard_map/ffn_dp1/ppermute | solution.py:37
  62.9 14.5 %collective-permute-start.16 = (bf16[256,1024]{1,0:T(8,128)(2,1)}, bf16[256,1024]{1,0:T(8,128)(2,1)S(1)}, u32[]{:S(2)}, u32[]{:S(2)}) collective-permute-start(bf16[256,1024]{1,0:T(8,128)(2,1)} %collective-permute-done.11.d_ref), channel_id=1, source_target_pairs={{0,1},{1,0},{2,3},{3,2},{4,5},{5,4},{6,7},{7,6},{8,9},{9,8},{10,11... | collective-permute-start | bytes 1572872 | tf_op jit(solution)/shard_map/dy_on_z1/ppermute | solution.py:49
  63.2 21.3 %collective-permute-start.6 = (bf16[544,1024]{1,0:T(8,128)(2,1)S(1)}, bf16[544,1024]{1,0:T(8,128)(2,1)}, u32[]{:S(2)}, u32[]{:S(2)}) collective-permute-start(bf16[544,1024]{1,0:T(8,128)(2,1)S(1)} %stack_mixer.1.refs_0_), channel_id=1, source_target_pairs={{0,4},{4,0},{8,12},{12,8},{16,20},{20,16},{24,28},{28,24},{1,5},{5... | collective-permute-start | bytes 3342344 | tf_op jit(solution)/shard_map/mix_dp1/ppermute | solution.py:37
  63.4 21.2 %collective-permute-start.10 = (bf16[544,1024]{1,0:T(8,128)(2,1)S(1)}, bf16[544,1024]{1,0:T(8,128)(2,1)}, u32[]{:S(2)}, u32[]{:S(2)}) collective-permute-start(bf16[544,1024]{1,0:T(8,128)(2,1)S(1)} %collective-permute-done.9.refs_4_), channel_id=1, source_target_pairs={{0,4},{4,0},{8,12},{12,8},{16,20},{20,16},{24,28},{28,24},{1,5},{5... | collective-permute-start | bytes 3342344 | tf_op jit(solution)/shard_map/mix_dp1/ppermute | solution.py:37
  78.2 6.4 %collective-permute-start.8 = (bf16[544,1024]{1,0:T(8,128)(2,1)S(1)}, bf16[544,1024]{1,0:T(8,128)(2,1)}, u32[]{:S(2)}, u32[]{:S(2)}) collective-permute-start(bf16[544,1024]{1,0:T(8,128)(2,1)S(1)} %collective-permute-done.7.refs_2_), channel_id=1, source_target_pairs={{0,4},{4,0},{8,12},{12,8},{16,20},{20,16},{24,28},{28,24},{1,5},{5... | collective-permute-start | bytes 3342344 | tf_op jit(solution)/shard_map/mix_dp1/ppermute | solution.py:37
  79.2 5.5 %collective-permute-start.17 = (bf16[544,1024]{1,0:T(8,128)(2,1)}, bf16[544,1024]{1,0:T(8,128)(2,1)}, u32[]{:S(2)}, u32[]{:S(2)}) collective-permute-start(bf16[544,1024]{1,0:T(8,128)(2,1)} %collective-permute-done.14.refs_6_), channel_id=1, source_target_pairs={{0,4},{4,0},{8,12},{12,8},{16,20},{20,16},{24,28},{28,24},{1,5},{5... | collective-permute-start | bytes 3342344 | tf_op jit(solution)/shard_map/mix_dp1/ppermute | solution.py:37
  81.9 13.4 %collective-permute-start.19 = (bf16[128,3456]{1,0:T(8,128)(2,1)}, bf16[128,3456]{1,0:T(8,128)(2,1)}, u32[]{:S(2)}, u32[]{:S(2)}) collective-permute-start(bf16[128,3456]{1,0:T(8,128)(2,1)} %broadcast_select_fusion.1), channel_id=1, source_target_pairs={{0,16},{4,12},{8,24},{12,4},{16,0},{20,28},{24,8},{28,20},{1,17},{... | collective-permute-start | bytes 2654216 | tf_op jit(solution)/shard_map/ffn_corner/ppermute | solution.py:97
  84.5 4.0 %copy-start.5 = (bf16[8,32,1024]{2,1,0:T(8,128)(2,1)S(1)}, bf16[8,32,1024]{2,1,0:T(8,128)(2,1)}, u32[]{:S(2)}) copy-start(bf16[8,32,1024]{2,1,0:T(8,128)(2,1)} %param.12) | copy-start | bytes 1572868
  84.5 13.6 %collective-permute-start.18 = (bf16[128,3456]{1,0:T(8,128)(2,1)}, bf16[128,3456]{1,0:T(8,128)(2,1)S(1)}, u32[]{:S(2)}, u32[]{:S(2)}) collective-permute-start(bf16[128,3456]{1,0:T(8,128)(2,1)} %copy-done.2), channel_id=1, source_target_pairs={{0,4},{4,0},{8,12},{12,8},{16,20},{20,16},{24,28},{28,24},{1,5},{5... | collective-permute-start | bytes 2654216 | tf_op jit(solution)/shard_map/ffn_dp1/ppermute | solution.py:37
  91.0 7.1 %copy-start.1 = (bf16[128,3456]{1,0:T(8,128)(2,1)S(1)}, bf16[128,3456]{1,0:T(8,128)(2,1)}, u32[]{:S(2)}) copy-start(bf16[128,3456]{1,0:T(8,128)(2,1)} %copy-done) | copy-start | bytes 2654212
  91.0 7.1 %copy-start.4 = (bf16[128,3456]{1,0:T(8,128)(2,1)S(1)}, bf16[128,3456]{1,0:T(8,128)(2,1)}, u32[]{:S(2)}) copy-start(bf16[128,3456]{1,0:T(8,128)(2,1)} %copy-done.2) | copy-start | bytes 2654212
  91.0 7.1 %copy-start.7 = (bf16[128,3456]{1,0:T(8,128)(2,1)S(1)}, bf16[128,3456]{1,0:T(8,128)(2,1)}, u32[]{:S(2)}) copy-start(bf16[128,3456]{1,0:T(8,128)(2,1)} %copy-done.6) | copy-start | bytes 2654212
  95.2 2.9 %collective-permute-start.20 = (bf16[128,3456]{1,0:T(8,128)(2,1)}, bf16[128,3456]{1,0:T(8,128)(2,1)S(1)}, u32[]{:S(2)}, u32[]{:S(2)}) collective-permute-start(bf16[128,3456]{1,0:T(8,128)(2,1)} %collective-permute-done.19.refs_6_), channel_id=1, source_target_pairs={{0,4},{4,0},{8,12},{12,8},{16,20},{20,16},{24,28},{28,24},{1,5},{5... | collective-permute-start | bytes 2654216 | tf_op jit(solution)/shard_map/ffn_dp1/ppermute | solution.py:37
  95.2 26.3 %collective-permute-start.22 = (bf16[256,1024]{1,0:T(8,128)(2,1)S(1)}, bf16[256,1024]{1,0:T(8,128)(2,1)S(1)}, u32[]{:S(2)}, u32[]{:S(2)}) collective-permute-start(bf16[256,1024]{1,0:T(8,128)(2,1)S(1)} %get-tuple-element.119.n_ref), channel_id=1, source_target_pairs={{0,2},{1,3},{2,0},{3,1},{4,6},{5,7},{6,4},{7,5},{8,10},{9,11},{10,... | collective-permute-start | bytes 1572872 | tf_op jit(solution)/shard_map/n2_z2/ppermute | solution.py:49
  96.4 25.3 %collective-permute-start.21 = (bf16[256,1024]{1,0:T(8,128)(2,1)S(1)}, bf16[256,1024]{1,0:T(8,128)(2,1)S(1)}, u32[]{:S(2)}, u32[]{:S(2)}) collective-permute-start(bf16[256,1024]{1,0:T(8,128)(2,1)S(1)} %get-tuple-element.119.n_ref), channel_id=1, source_target_pairs={{0,1},{1,0},{2,3},{3,2},{4,5},{5,4},{6,7},{7,6},{8,9},{9,8},{10,11... | collective-permute-start | bytes 1572872 | tf_op jit(solution)/shard_map/n2_z1/ppermute | solution.py:49
  121.5 13.8 %collective-permute-start.23 = (bf16[256,1024]{1,0:T(8,128)(2,1)S(1)}, bf16[256,1024]{1,0:T(8,128)(2,1)S(1)}, u32[]{:S(2)}, u32[]{:S(2)}) collective-permute-start(bf16[256,1024]{1,0:T(8,128)(2,1)S(1)} %collective-permute-done.22.n_ref), channel_id=1, source_target_pairs={{0,1},{1,0},{2,3},{3,2},{4,5},{5,4},{6,7},{7,6},{8,9},{9,8},{10,11... | collective-permute-start | bytes 1572872 | tf_op jit(solution)/shard_map/n2_on_z1/ppermute | solution.py:49
  128.8 6.6 %copy-start.9 = (bf16[256,1024]{1,0:T(8,128)(2,1)S(1)}, bf16[256,1024]{1,0:T(8,128)(2,1)}, u32[]{:S(2)}) copy-start(bf16[256,1024]{1,0:T(8,128)(2,1)} %copy-done.8) | copy-start | bytes 1572868
  139.7 14.9 %collective-permute-start.29 = (bf16[256,1024]{1,0:T(8,128)(2,1)S(1)}, bf16[256,1024]{1,0:T(8,128)(2,1)S(1)}, u32[]{:S(2)}, u32[]{:S(2)}) collective-permute-start(bf16[256,1024]{1,0:T(8,128)(2,1)S(1)} %get-tuple-element.152), channel_id=1, source_target_pairs={{0,1},{1,0},{2,3},{3,2},{4,5},{5,4},{6,7},{7,6},{8,9},{9,8},{10,11... | collective-permute-start | bytes 1572872 | tf_op jit(solution)/shard_map/dn_on_z1/ppermute | solution.py:49
  140.6 34.1 %collective-permute-start.24 = (bf16[256,1024]{1,0:T(8,128)(2,1)S(1)}, bf16[256,1024]{1,0:T(8,128)(2,1)S(1)}, u32[]{:S(2)}, u32[]{:S(2)}) collective-permute-start(bf16[256,1024]{1,0:T(8,128)(2,1)S(1)} %get-tuple-element.132), channel_id=1, source_target_pairs={{0,1},{1,0},{2,3},{3,2},{4,5},{5,4},{6,7},{7,6},{8,9},{9,8},{10,11... | collective-permute-start | bytes 1572872 | tf_op jit(solution)/shard_map/dn_z1/ppermute | solution.py:49
  154.8 22.2 %collective-permute-start.30 = (bf16[256,1024]{1,0:T(8,128)(2,1)S(1)}, bf16[256,1024]{1,0:T(8,128)(2,1)S(1)}, u32[]{:S(2)}, u32[]{:S(2)}) collective-permute-start(bf16[256,1024]{1,0:T(8,128)(2,1)S(1)} %add_convert_fusion.12), channel_id=1, source_target_pairs={{0,2},{1,3},{2,0},{3,1},{4,6},{5,7},{6,4},{7,5},{8,10},{9,11},{10,... | collective-permute-start | bytes 1572872 | tf_op jit(solution)/shard_map/dn_z2/ppermute | solution.py:49
  156.4 27.2 %collective-permute-start.28 = (bf16[4,128,3456]{2,1,0:T(8,128)(2,1)S(1)}, bf16[4,128,3456]{2,1,0:T(8,128)(2,1)S(1)}, u32[]{:S(2)}, u32[]{:S(2)}) collective-permute-start(bf16[4,128,3456]{2,1,0:T(8,128)(2,1)S(1)} %get-tuple-element.150), channel_id=1, source_target_pairs={{0,4},{4,0},{8,12},{12,8},{16,20},{20,16},{24,28},{28,24},{1,5},{5... | collective-permute-start | bytes 10616840 | tf_op jit(solution)/shard_map/gf_dp1/ppermute | solution.py:37
  174.7 12.7 %collective-permute-start.26 = (bf16[256,1024]{1,0:T(8,128)(2,1)S(1)}, bf16[256,1024]{1,0:T(8,128)(2,1)S(1)}, u32[]{:S(2)}, u32[]{:S(2)}) collective-permute-start(bf16[256,1024]{1,0:T(8,128)(2,1)S(1)} %get-tuple-element.144), channel_id=1, source_target_pairs={{0,1},{1,0},{2,3},{3,2},{4,5},{5,4},{6,7},{7,6},{8,9},{9,8},{10,11... | collective-permute-start | bytes 1572872 | tf_op jit(solution)/shard_map/out_on_z1/ppermute | solution.py:49
  187.4 4.2 %collective-permute-start.31 = (bf16[4,256,1024]{2,1,0:T(8,128)(2,1)S(1)}, bf16[4,256,1024]{2,1,0:T(8,128)(2,1)S(1)}, u32[]{:S(2)}, u32[]{:S(2)}) collective-permute-start(bf16[4,256,1024]{2,1,0:T(8,128)(2,1)S(1)} %get-tuple-element.177), channel_id=1, source_target_pairs={{0,4},{4,0},{8,12},{12,8},{16,20},{20,16},{24,28},{28,24},{1,5},{5... | collective-permute-start | bytes 6291464 | tf_op jit(solution)/shard_map/gco_dp1/ppermute | solution.py:37
  192.0 4.7 %collective-permute-start.32 = (bf16[4,288,1024]{2,1,0:T(8,128)(2,1)S(1)}, bf16[4,288,1024]{2,1,0:T(8,128)(2,1)S(1)}, u32[]{:S(2)}, u32[]{:S(2)}) collective-permute-start(bf16[4,288,1024]{2,1,0:T(8,128)(2,1)S(1)} %get-tuple-element.178), channel_id=1, source_target_pairs={{0,4},{4,0},{8,12},{12,8},{16,20},{20,16},{24,28},{28,24},{1,5},{5... | collective-permute-start | bytes 7077896 | tf_op jit(solution)/shard_map/gbu_dp1/ppermute | solution.py:37
  192.5 9.9 %collective-permute-start.33 = (bf16[256,1024]{1,0:T(8,128)(2,1)S(1)}, bf16[256,1024]{1,0:T(8,128)(2,1)S(1)}, u32[]{:S(2)}, u32[]{:S(2)}) collective-permute-start(bf16[256,1024]{1,0:T(8,128)(2,1)S(1)} %get-tuple-element.234), channel_id=1, source_target_pairs={{0,16},{4,12},{8,24},{12,4},{16,0},{20,28},{24,8},{28,20},{1,17},{... | collective-permute-start | bytes 1572872 | tf_op jit(solution)/shard_map/gco_corner/ppermute | solution.py:97
  197.1 14.0 %collective-permute-start.36 = (bf16[288,1024]{1,0:T(8,128)(2,1)S(1)}, bf16[288,1024]{1,0:T(8,128)(2,1)S(1)}, u32[]{:S(2)}, u32[]{:S(2)}) collective-permute-start(bf16[288,1024]{1,0:T(8,128)(2,1)S(1)} %get-tuple-element.230), channel_id=1, source_target_pairs={{0,16},{4,12},{8,24},{12,4},{16,0},{20,28},{24,8},{28,20},{1,17},{... | collective-permute-start | bytes 1769480 | tf_op jit(solution)/shard_map/gbu_corner/ppermute | solution.py:97
  198.7 26.2 %collective-permute-start.45 = (bf16[128,3456]{1,0:T(8,128)(2,1)S(1)}, bf16[128,3456]{1,0:T(8,128)(2,1)S(1)}, u32[]{:S(2)}, u32[]{:S(2)}) collective-permute-start(bf16[128,3456]{1,0:T(8,128)(2,1)S(1)} %fusion.13), channel_id=1, source_target_pairs={{0,16},{4,12},{8,24},{12,4},{16,0},{20,28},{24,8},{28,20},{1,17},{... | collective-permute-start | bytes 2654216 | tf_op jit(solution)/shard_map/gf_corner/ppermute | solution.py:97
  199.2 24.1 %collective-permute-start.25 = (bf16[256,1024]{1,0:T(8,128)(2,1)S(1)}, bf16[256,1024]{1,0:T(8,128)(2,1)S(1)}, u32[]{:S(2)}, u32[]{:S(2)}) collective-permute-start(bf16[256,1024]{1,0:T(8,128)(2,1)S(1)} %get-tuple-element.133), channel_id=1, source_target_pairs={{0,1},{1,0},{2,3},{3,2},{4,5},{5,4},{6,7},{7,6},{8,9},{9,8},{10,11... | collective-permute-start | bytes 1572872 | tf_op jit(solution)/shard_map/out_z1/ppermute | solution.py:49
  200.1 26.0 %collective-permute-start.27 = (bf16[256,1024]{1,0:T(8,128)(2,1)S(1)}, bf16[256,1024]{1,0:T(8,128)(2,1)S(1)}, u32[]{:S(2)}, u32[]{:S(2)}) collective-permute-start(bf16[256,1024]{1,0:T(8,128)(2,1)S(1)} %add_convert_fusion.14), channel_id=1, source_target_pairs={{0,2},{1,3},{2,0},{3,1},{4,6},{5,7},{6,4},{7,5},{8,10},{9,11},{10,... | collective-permute-start | bytes 1572872 | tf_op jit(solution)/shard_map/out_z2/ppermute | solution.py:49
  203.0 29.5 %collective-permute-start.35 = (bf16[256,1024]{1,0:T(8,128)(2,1)S(1)}, bf16[256,1024]{1,0:T(8,128)(2,1)S(1)}, u32[]{:S(2)}, u32[]{:S(2)}) collective-permute-start(bf16[256,1024]{1,0:T(8,128)(2,1)S(1)} %get-tuple-element.232), channel_id=1, source_target_pairs={{0,16},{4,20},{8,24},{12,28},{16,0},{20,4},{24,8},{28,12},{1,17},{... | collective-permute-start | bytes 1572872 | tf_op jit(solution)/shard_map/gco_dp4/ppermute | solution.py:37
  211.1 22.9 %collective-permute-start.34 = (bf16[256,1024]{1,0:T(8,128)(2,1)S(1)}, bf16[256,1024]{1,0:T(8,128)(2,1)S(1)}, u32[]{:S(2)}, u32[]{:S(2)}) collective-permute-start(bf16[256,1024]{1,0:T(8,128)(2,1)S(1)} %get-tuple-element.233), channel_id=1, source_target_pairs={{0,8},{4,12},{8,0},{12,4},{16,24},{20,28},{24,16},{28,20},{1,9},{5... | collective-permute-start | bytes 1572872 | tf_op jit(solution)/shard_map/gco_dp2/ppermute | solution.py:37
  223.4 21.8 %collective-permute-start.38 = (bf16[288,1024]{1,0:T(8,128)(2,1)S(1)}, bf16[288,1024]{1,0:T(8,128)(2,1)S(1)}, u32[]{:S(2)}, u32[]{:S(2)}) collective-permute-start(bf16[288,1024]{1,0:T(8,128)(2,1)S(1)} %get-tuple-element.228), channel_id=1, source_target_pairs={{0,16},{4,20},{8,24},{12,28},{16,0},{20,4},{24,8},{28,12},{1,17},{... | collective-permute-start | bytes 1769480 | tf_op jit(solution)/shard_map/gbu_dp4/ppermute | solution.py:37
  224.9 22.9 %collective-permute-start.37 = (bf16[288,1024]{1,0:T(8,128)(2,1)S(1)}, bf16[288,1024]{1,0:T(8,128)(2,1)S(1)}, u32[]{:S(2)}, u32[]{:S(2)}) collective-permute-start(bf16[288,1024]{1,0:T(8,128)(2,1)S(1)} %get-tuple-element.229), channel_id=1, source_target_pairs={{0,8},{4,12},{8,0},{12,4},{16,24},{20,28},{24,16},{28,20},{1,9},{5... | collective-permute-start | bytes 1769480 | tf_op jit(solution)/shard_map/gbu_dp2/ppermute | solution.py:37
  226.1 43.1 %collective-permute-start.46 = (bf16[128,3456]{1,0:T(8,128)(2,1)S(1)}, bf16[128,3456]{1,0:T(8,128)(2,1)S(1)}, u32[]{:S(2)}, u32[]{:S(2)}) collective-permute-start(bf16[128,3456]{1,0:T(8,128)(2,1)S(1)} %get-tuple-element.195), channel_id=1, source_target_pairs={{0,8},{4,12},{8,0},{12,4},{16,24},{20,28},{24,16},{28,20},{1,9},{5... | collective-permute-start | bytes 2654216 | tf_op jit(solution)/shard_map/gf_dp2/ppermute | solution.py:37
  232.5 36.8 %collective-permute-start.47 = (bf16[128,3456]{1,0:T(8,128)(2,1)S(1)}, bf16[128,3456]{1,0:T(8,128)(2,1)S(1)}, u32[]{:S(2)}, u32[]{:S(2)}) collective-permute-start(bf16[128,3456]{1,0:T(8,128)(2,1)S(1)} %get-tuple-element.196), channel_id=1, source_target_pairs={{0,16},{4,20},{8,24},{12,28},{16,0},{20,4},{24,8},{28,12},{1,17},{... | collective-permute-start | bytes 2654216 | tf_op jit(solution)/shard_map/gf_dp4/ppermute | solution.py:37
  234.8 15.4 %collective-permute-start.42 = (bf16[256,256]{1,0:T(8,128)(2,1)S(1)}, bf16[256,256]{1,0:T(8,128)(2,1)S(1)}, u32[]{:S(2)}, u32[]{:S(2)}) collective-permute-start(bf16[256,256]{1,0:T(8,128)(2,1)S(1)} %get-tuple-element.186), channel_id=1, source_target_pairs={{0,1},{1,0},{2,3},{3,2},{4,5},{5,4},{6,7},{7,6},{8,9},{9,8},{10,11... | collective-permute-start | bytes 393224 | tf_op jit(solution)/shard_map/gco_z1/ppermute | solution.py:49
  245.2 12.3 %collective-permute-start.43 = (bf16[256,256]{1,0:T(8,128)(2,1)S(1)}, bf16[256,256]{1,0:T(8,128)(2,1)S(1)}, u32[]{:S(2)}, u32[]{:S(2)}) collective-permute-start(bf16[256,256]{1,0:T(8,128)(2,1)S(1)} %get-tuple-element.187), channel_id=1, source_target_pairs={{0,2},{1,3},{2,0},{3,1},{4,6},{5,7},{6,4},{7,5},{8,10},{9,11},{10,... | collective-permute-start | bytes 393224 | tf_op jit(solution)/shard_map/gco_z2/ppermute | solution.py:49
  247.8 9.6 %collective-permute-start.44 = (bf16[256,256]{1,0:T(8,128)(2,1)S(1)}, bf16[256,256]{1,0:T(8,128)(2,1)S(1)}, u32[]{:S(2)}, u32[]{:S(2)}) collective-permute-start(bf16[256,256]{1,0:T(8,128)(2,1)S(1)} %get-tuple-element.188), channel_id=1, source_target_pairs={{0,3},{1,2},{2,1},{3,0},{4,7},{5,6},{6,5},{7,4},{8,11},{9,10},{10,... | collective-permute-start | bytes 393224 | tf_op jit(solution)/shard_map/gco_z3/ppermute | solution.py:49
  250.2 11.6 %collective-permute-start.39 = (bf16[336,256]{1,0:T(8,128)(2,1)S(1)}, bf16[336,256]{1,0:T(8,128)(2,1)S(1)}, u32[]{:S(2)}, u32[]{:S(2)}) collective-permute-start(bf16[336,256]{1,0:T(8,128)(2,1)S(1)} %get-tuple-element.183), channel_id=1, source_target_pairs={{0,1},{1,0},{2,3},{3,2},{4,5},{5,4},{6,7},{7,6},{8,9},{9,8},{10,11... | collective-permute-start | bytes 516104 | tf_op jit(solution)/shard_map/gbu_z1/ppermute | solution.py:49
  257.5 9.5 %collective-permute-start.40 = (bf16[336,256]{1,0:T(8,128)(2,1)S(1)}, bf16[336,256]{1,0:T(8,128)(2,1)S(1)}, u32[]{:S(2)}, u32[]{:S(2)}) collective-permute-start(bf16[336,256]{1,0:T(8,128)(2,1)S(1)} %get-tuple-element.184), channel_id=1, source_target_pairs={{0,2},{1,3},{2,0},{3,1},{4,6},{5,7},{6,4},{7,5},{8,10},{9,11},{10,... | collective-permute-start | bytes 516104 | tf_op jit(solution)/shard_map/gbu_z2/ppermute | solution.py:49
  257.5 9.5 %collective-permute-start.41 = (bf16[336,256]{1,0:T(8,128)(2,1)S(1)}, bf16[336,256]{1,0:T(8,128)(2,1)S(1)}, u32[]{:S(2)}, u32[]{:S(2)}) collective-permute-start(bf16[336,256]{1,0:T(8,128)(2,1)S(1)} %get-tuple-element.185), channel_id=1, source_target_pairs={{0,3},{1,2},{2,1},{3,0},{4,7},{5,6},{6,5},{7,4},{8,11},{9,10},{10,... | collective-permute-start | bytes 516104 | tf_op jit(solution)/shard_map/gbu_z3/ppermute | solution.py:49
  (5 other events, 4.4 us)
where the time goes:
time: 274 us; the launch traced here: 273 us
  waiting for transfers between devices  138 us (50%)
  Pallas kernels  60.5 us (22%)
  starting transfers between devices  49.1 us (18%)
  local copies, waits for them, and re-layouts  13.4 us (5%)
  other arithmetic  9.97 us (4%)
    ppermute x21, waiting for transfers between devices, z_swap(): return lax.ppermute(value, 'tensor', [(i, i ^ step) for i in range(size)])  91.4 us
    pallas_call x17, Pallas kernels, whole_call(): pl.pallas_call(kernel, out_shape=outs, in_specs=specs, out_specs=[pl.Bloc...  60.5 us
    ppermute x21, waiting for transfers between devices, dp_swap(): return lax.ppermute(value, 'dp', [(i, i ^ hop) for i in range(size)])  37.4 us
    ppermute x21, starting transfers between devices, z_swap(): return lax.ppermute(value, 'tensor', [(i, i ^ step) for i in range(size)])  28.4 us
    ppermute x21, starting transfers between devices, dp_swap(): return lax.ppermute(value, 'dp', [(i, i ^ hop) for i in range(size)])  14.6 us
    ppermute x5, waiting for transfers between devices, corner(): return lax.ppermute(value, 'dp', pairs)  9.32 us
    unnamed x48, local copies, waits for them, and re-layouts  8 us
    ppermute x5, starting transfers between devices, corner(): return lax.ppermute(value, 'dp', pairs)  5.63 us
  transfers between devices with their start and end apart: 48, of which 24 were waited for; matrix products, arithmetic and copies ran while one was open for 4% of the time, Pallas kernels for 21%

commit v1 on v0

--- a/solution.py
+++ b/solution.py
@@ -702,7 +702,7 @@
     )
     c_own, gated, middle, n_two = mixer_out(x_own, n_one, conv, small_all, w_c, w_o)
 
-    ffn_d = plane_corner(ffn_x, ffn_y, "ffn", mix_d)
+    ffn_d = plane_corner(ffn_x, ffn_y, "ffn", dy_far)
     n_two_far, n_two_near = z_send(n_two, "n2", (2, 1))
     n_two_set = [n_two, n_two_near, n_two_far]
     ffn_pairs += [ffn_d, dp_swap(after(ffn_d, n_two), 1, "ffn")]
@@ -743,7 +743,7 @@
     out_second = z_swap(out_second, 2, "out")
     co_across = plane_far(co_pieces, "gco")
     co_terms = plane_near(co_pieces, co_across, "gco")
-    bu_pieces = core_sum(after(bu_away, co_pieces[0]), bu_home, 4, "gbu")
+    bu_pieces = core_sum(bu_away, bu_home, 4, "gbu")
     bu_across = plane_far(bu_pieces, "gbu")
     bu_terms = plane_near(bu_pieces, bu_across, "gbu")
     ffn_terms = plane_near(ffn_pieces, ffn_across, "gf", bu_across)
@@ -755,7 +755,7 @@
         parts = split_z(index, (first, *terms[1:]), 2 * block, n_z)
         return [parts[0]] + [z_swap(parts[s], s, tag) for s in range(1, n_z)]
 
-    co_parts = z_parts(co_terms, "gco", out_first, out_second)
+    co_parts = z_parts(co_terms, "gco", out_second)
     ffn_total = sum(term.astype(F32) for term in ffn_terms)
     if outer > 1:
         narrow = functools.partial(

time: 274 us -> 272 us (level)
  starting transfers between devices: 49.1 us -> 44.9 us
  waiting for transfers between devices: 138 us -> 141 us
    ppermute x21, starting transfers between devices: 28.4 us -> 25.2 us  [z_swap(): return lax.ppermute(value, 'tensor', [(i, i ^ step) for i in range(size)])]
  transfers between devices with their start and end apart: 48 -> 48, of which waited for: 24 -> 24; matrix products, arithmetic and copies ran while one was open for 4% -> 5% of each run, Pallas kernels for 21% -> 21%
where the time goes in v1:
time: 272 us
  waiting for transfers between devices  141 us (52%)
  Pallas kernels  60.5 us (22%)
  starting transfers between devices  44.9 us (17%)
  local copies, waits for them, and re-layouts  13.4 us (5%)
  other arithmetic  9.97 us (4%)
    ppermute x21, waiting for transfers between devices, z_swap(): return lax.ppermute(value, 'tensor', [(i, i ^ step) for i in range(size)])  92.2 us
    pallas_call x17, Pallas kernels, whole_call(): pl.pallas_call(kernel, out_shape=outs, in_specs=specs, out_specs=[pl.Bloc...  60.5 us
    ppermute x21, waiting for transfers between devices, dp_swap(): return lax.ppermute(value, 'dp', [(i, i ^ hop) for i in range(size)])  38.6 us
    ppermute x21, starting transfers between devices, z_swap(): return lax.ppermute(value, 'tensor', [(i, i ^ step) for i in range(size)])  25.2 us
    ppermute x21, starting transfers between devices, dp_swap(): return lax.ppermute(value, 'dp', [(i, i ^ hop) for i in range(size)])  13.6 us
    ppermute x5, waiting for transfers between devices, corner(): return lax.ppermute(value, 'dp', pairs)  10.3 us
    unnamed x48, local copies, waits for them, and re-layouts  8 us
    ppermute x5, starting transfers between devices, corner(): return lax.ppermute(value, 'dp', pairs)  5.69 us
  transfers between devices with their start and end apart: 48, of which 24 were waited for; matrix products, arithmetic and copies ran while one was open for 5% of the time, Pallas kernels for 21%

profile of v1, /device:TPU:0, one launch (start us, length us, event | category | flops | bytes accessed | tf_op | source)
XLA Modules:
  0.0 271.7 jit_solution(16699482788753376669)
XLA Ops:
  0.7 1.0 fusion.41
  4.4 4.1 %collective-permute-start.2 = (bf16[512,256]{1,0:T(8,128)(2,1)S(1)}, bf16[512,256]{1,0:T(8,128)(2,1)S(1)}, u32[]{:S(2)}, u32[]{:S(2)}) collective-permute-start(bf16[512,256]{1,0:T(8,128)(2,1)S(1)} %bitcast.84), channel_id=1, source_target_pairs={{0,2},{1,3},{2,0},{3,1},{4,6},{5,7},{6,4},{7,5},{8,10},{9,11},{10,... | collective-permute-start | bytes 786440 | tf_op jit(solution)/shard_map/mix_z2/ppermute | solution.py:49
  8.5 1.6 collective-permute-start.1
  10.1 1.5 collective-permute-start.5
  11.6 1.5 collective-permute-start.4
  13.1 0.9 slice.108
  15.4 5.1 %collective-permute-done.2.refs_2_ = bf16[512,256]{1,0:T(8,128)(2,1)S(1)} collective-permute-done((bf16[512,256]{1,0:T(8,128)(2,1)S(1)}, bf16[512,256]{1,0:T(8,128)(2,1)S(1)}, u32[]{:S(2)}, u32[]{:S(2)}) %collective-permute-start.2) | collective-permute-done | bytes 262176 | tf_op jit(solution)/shard_map/mix_z2/ppermute | solution.py:49
  22.9 5.0 %collective-permute-done.3.refs_3_ = bf16[512,256]{1,0:T(8,128)(2,1)S(1)} collective-permute-done((bf16[512,256]{1,0:T(8,128)(2,1)S(1)}, bf16[512,256]{1,0:T(8,128)(2,1)S(1)}, u32[]{:S(2)}, u32[]{:S(2)}) %collective-permute-start.3) | collective-permute-done | bytes 262176 | tf_op jit(solution)/shard_map/mix_on_z1/ppermute | solution.py:49
  27.9 0.9 copy-done.11
  29.6 1.3 collective-permute-done.5.refs_4_
  30.9 1.0 copy-done.2
  32.2 1.2 collective-permute-start.9
  33.4 1.5 collective-permute-start.7
  35.4 3.1 %collective-permute-start.11 = (bf16[256,1024]{1,0:T(8,128)(2,1)}, bf16[256,1024]{1,0:T(8,128)(2,1)}, u32[]{:S(2)}, u32[]{:S(2)}) collective-permute-start(bf16[256,1024]{1,0:T(8,128)(2,1)} %bitcast.7.d_ref.refs_4_), channel_id=1, source_target_pairs={{0,2},{1,3},{2,0},{3,1},{4,6},{5,7},{6,4},{7,5},{8,10},{9,11},{10,... | collective-permute-start | bytes 1572872 | tf_op jit(solution)/shard_map/dy_z2/ppermute | solution.py:49
  38.4 18.5 %collective-permute-done.9.refs_4_ = bf16[544,1024]{1,0:T(8,128)(2,1)S(1)} collective-permute-done((bf16[544,1024]{1,0:T(8,128)(2,1)S(1)}, bf16[544,1024]{1,0:T(8,128)(2,1)S(1)}, u32[]{:S(2)}, u32[]{:S(2)}) %collective-permute-start.9) | collective-permute-done | bytes 1114144 | tf_op jit(solution)/shard_map/mix_dp4/ppermute | solution.py:37
  56.9 1.2 collective-permute-done.7.refs_2_
  58.3 2.3 collective-permute-done.12.d_ref
  60.6 1.8 collective-permute-done.11.d_ref
  63.7 13.7 %collective-permute-done.16.d_ref = bf16[256,1024]{1,0:T(8,128)(2,1)S(1)} collective-permute-done((bf16[256,1024]{1,0:T(8,128)(2,1)}, bf16[256,1024]{1,0:T(8,128)(2,1)S(1)}, u32[]{:S(2)}, u32[]{:S(2)}) %collective-permute-start.16) | collective-permute-done | bytes 524320 | tf_op jit(solution)/shard_map/dy_on_z1/ppermute | solution.py:49
  78.2 0.9 copy-done.6
  79.7 2.2 broadcast_select_fusion.1
  81.9 1.5 collective-permute-start.19
  84.6 3.7 %place_mixer.1 = (bf16[1024,1024]{1,0:T(8,128)(2,1)S(1)}, bf16[1024,1024]{1,0:T(8,128)(2,1)S(1)}, bf16[1024,1024]{1,0:T(8,128)(2,1)S(1)}, bf16[1024,1024]{1,0:T(...) custom-call(s32[2]{0:T(128)S(1)} %pad_add_fusion.idx_ref, ...), custom_call_target="tpu_custom_call" | custom-call | flops 1 | bytes 1 | tf_op jit(solution)/shard_map/place_mixer/pallas_call | solution.py:76
  88.5 2.4 mixer_in.1
  91.0 1.4 mixer_out.1
  92.4 2.8 %collective-permute-done.19.refs_6_ = bf16[128,3456]{1,0:T(8,128)(2,1)} collective-permute-done((bf16[128,3456]{1,0:T(8,128)(2,1)}, bf16[128,3456]{1,0:T(8,128)(2,1)}, u32[]{:S(2)}, u32[]{:S(2)}) %collective-permute-start.19) | collective-permute-done | bytes 884768 | tf_op jit(solution)/shard_map/ffn_corner/ppermute | solution.py:97
  95.2 1.1 collective-permute-start.22
  96.4 1.7 collective-permute-start.21
  98.1 2.7 place_ffn.1.w_ref
  100.8 7.0 %ffn_piece.4 = (bf16[256,1024]{1,0:T(8,128)(2,1)S(1)}, bf16[256,1024]{1,0:T(8,128)(2,1)S(1)}, bf16[1024,1024]{1,0:T(8,128)(2,1)S(1)}, bf16[1024,1024]{1,0:T(8,12...) custom-call(bf16[256,1024]{1,0:T(8,128)(2,1)S(1)} %get-tuple-element.118.n_ref, ...), custom_call_target="tpu_custom_call" | custom-call | flops 1 | bytes 1 | tf_op jit(solution)/shard_map/ffn_piece/pallas_call | solution.py:76
  107.8 13.8 %collective-permute-done.22.n_ref = bf16[256,1024]{1,0:T(8,128)(2,1)S(1)} collective-permute-done((bf16[256,1024]{1,0:T(8,128)(2,1)S(1)}, bf16[256,1024]{1,0:T(8,128)(2,1)S(1)}, u32[]{:S(2)}, u32[]{:S(2)}) %collective-permute-start.22) | collective-permute-done | bytes 524320 | tf_op jit(solution)/shard_map/n2_z2/ppermute | solution.py:49
  121.7 7.1 %ffn_piece.5 = (bf16[256,1024]{1,0:T(8,128)(2,1)S(1)}, bf16[256,1024]{1,0:T(8,128)(2,1)S(1)}, bf16[1024,1024]{1,0:T(8,128)(2,1)S(1)}, bf16[1024,1024]{1,0:T(8,12...) custom-call(bf16[256,1024]{1,0:T(8,128)(2,1)S(1)} %collective-permut, ...), custom_call_target="tpu_custom_call", output_to_operand_aliasing={{2}: (3, {}), {3}: (4, {}), {4}: (5, {}), {5}: (6, {})} | custom-call | flops 1 | bytes 1 | tf_op jit(solution)/shard_map/ffn_piece/pallas_call | solution.py:76
  128.8 5.5 %ffn_piece.6 = (bf16[256,1024]{1,0:T(8,128)(2,1)S(1)}, bf16[256,1024]{1,0:T(8,128)(2,1)S(1)}, bf16[1024,1024]{1,0:T(8,128)(2,1)S(1)}, bf16[1024,1024]{1,0:T(8,12...) custom-call(bf16[256,1024]{1,0:T(8,128)(2,1)S(1)} %collective-permut, ...), custom_call_target="tpu_custom_call", output_to_operand_aliasing={{2}: (3, {}), {3}: (4, {}), {4}: (5, {}), {5}: (6, {})} | custom-call | flops 1 | bytes 1 | tf_op jit(solution)/shard_map/ffn_piece/pallas_call | solution.py:76
  134.3 1.1 collective-permute-done.23.n_ref
  135.4 4.4 %ffn_piece.7 = (bf16[256,1024]{1,0:T(8,128)(2,1)S(1)}, bf16[256,1024]{1,0:T(8,128)(2,1)S(1)}, bf16[1024,1024]{1,0:T(8,128)(2,1)S(1)}, bf16[1024,1024]{1,0:T(8,12...) custom-call(bf16[256,1024]{1,0:T(8,128)(2,1)S(1)} %collective-permut, ...), custom_call_target="tpu_custom_call", output_to_operand_aliasing={{2}: (3, {}), {3}: (4, {}), {4}: (5, {}), {5}: (6, {})} | custom-call | flops 1 | bytes 1 | tf_op jit(solution)/shard_map/ffn_piece/pallas_call | solution.py:76
  140.6 1.2 collective-permute-start.24
  141.8 9.4 %ffn_grads.1 = (bf16[4,128,3456]{2,1,0:T(8,128)(2,1)S(1)}, bf16[4,128,3456]{2,1,0:T(8,128)(2,1)S(1)}) custom-call(s32[2]{0:T(128)S(1)} %pad_add_fusion.idx_ref, bf16[1024,1024]{1,0:T(8,128)(2,1)S(1)} %get-tuple-element.144.n_ref, bf16[1024,1024]{1,0:T(8,128)(2,1)S(1)} %get-tuple-element.145.d_ref, bf16[1024,1152]{1,0:T(8,128)(2,1)S(1)} %get-tuple-element.146.hid_ref, ...), custom_call_target="tpu_custom_call" | custom-call | flops 1 | bytes 1 | tf_op jit(solution)/shard_map/ffn_grads/pallas_call | solution.py:76
  151.2 3.4 %collective-permute-done.29 = bf16[256,1024]{1,0:T(8,128)(2,1)S(1)} collective-permute-done((bf16[256,1024]{1,0:T(8,128)(2,1)S(1)}, bf16[256,1024]{1,0:T(8,128)(2,1)S(1)}, u32[]{:S(2)}, u32[]{:S(2)}) %collective-permute-start.29) | collective-permute-done | bytes 524320 | tf_op jit(solution)/shard_map/dn_on_z1/ppermute | solution.py:49
  154.8 1.6 collective-permute-start.30
  156.5 18.3 %collective-permute-done.24.refs_1_ = bf16[256,1024]{1,0:T(8,128)(2,1)S(1)} collective-permute-done((bf16[256,1024]{1,0:T(8,128)(2,1)S(1)}, bf16[256,1024]{1,0:T(8,128)(2,1)S(1)}, u32[]{:S(2)}, u32[]{:S(2)}) %collective-permute-start.24) | collective-permute-done | bytes 524320 | tf_op jit(solution)/shard_map/dn_z1/ppermute | solution.py:49
  174.7 2.3 collective-permute-done.30.refs_2_
  177.0 6.6 %mixer_back.1 = (bf16[256,1024]{1,0:T(8,128)(2,1)S(1)}, bf16[256,1024]{1,0:T(8,128)(2,1)S(1)}, bf16[256,1024]{1,0:T(8,128)(2,1)S(1)}, bf16[256,1024]{1,0:T(8,128...) custom-call(bf16[256,1024]{1,0:T(8,128)(2,1)S(1)} %get-tuple-element, ...), custom_call_target="tpu_custom_call" | custom-call | flops 60000002048 | bytes 1 | tf_op jit(solution)/shard_map/mixer_back/pallas_call | solution.py:76
  184.2 2.5 grads_out.1
  187.4 3.8 %grads_in.1 = (bf16[4,288,1024]{2,1,0:T(8,128)(2,1)S(1)}, bf16[4,288,1024]{2,1,0:T(8,128)(2,1)S(1)}) custom-call(s32[2]{0:T(128)S(1)} %pad_add_fusion.idx_ref, bf16[256,1024]{1,0:T(8,128)(2,1)S(1)} %get-tuple-element.165.n_ref.refs_0_.refs_2_, bf16[256,1024]{1,0:T(8,128)(2,1)S(1)} %get-tuple-element.166.refs_1_, ...), custom_call_target="tpu_custom_call" | custom-call | flops 1 | bytes 1 | tf_op jit(solution)/shard_map/grads_in/pallas_call | solution.py:76
  192.2 1.6 collective-permute-start.33
  193.7 2.2 collective-permute-done.31
  196.4 1.6 collective-permute-start.36
  198.5 1.0 collective-permute-start.25
  199.7 2.0 collective-permute-start.27
  202.2 1.6 collective-permute-start.35
  203.8 7.5 %collective-permute-done.36 = bf16[288,1024]{1,0:T(8,128)(2,1)S(1)} collective-permute-done((bf16[288,1024]{1,0:T(8,128)(2,1)S(1)}, bf16[288,1024]{1,0:T(8,128)(2,1)S(1)}, u32[]{:S(2)}, u32[]{:S(2)}) %collective-permute-start.36) | collective-permute-done | bytes 589856 | tf_op jit(solution)/shard_map/gbu_corner/ppermute | solution.py:97
  212.5 12.8 %collective-permute-done.27 = bf16[256,1024]{1,0:T(8,128)(2,1)S(1)} collective-permute-done((bf16[256,1024]{1,0:T(8,128)(2,1)S(1)}, bf16[256,1024]{1,0:T(8,128)(2,1)S(1)}, u32[]{:S(2)}, u32[]{:S(2)}) %collective-permute-start.27) | collective-permute-done | bytes 524320 | tf_op jit(solution)/shard_map/out_z2/ppermute | solution.py:49
  225.3 1.5 collective-permute-start.38
  228.1 5.3 %collective-permute-done.35.refs_2_ = bf16[256,1024]{1,0:T(8,128)(2,1)S(1)} collective-permute-done((bf16[256,1024]{1,0:T(8,128)(2,1)S(1)}, bf16[256,1024]{1,0:T(8,128)(2,1)S(1)}, u32[]{:S(2)}, u32[]{:S(2)}) %collective-permute-start.35) | collective-permute-done | bytes 524320 | tf_op jit(solution)/shard_map/gco_dp4/ppermute | solution.py:37
  233.9 1.5 collective-permute-start.47
  236.3 9.7 %collective-permute-done.38.refs_2_ = bf16[288,1024]{1,0:T(8,128)(2,1)S(1)} collective-permute-done((bf16[288,1024]{1,0:T(8,128)(2,1)S(1)}, bf16[288,1024]{1,0:T(8,128)(2,1)S(1)}, u32[]{:S(2)}, u32[]{:S(2)}) %collective-permute-start.38) | collective-permute-done | bytes 589856 | tf_op jit(solution)/shard_map/gbu_dp4/ppermute | solution.py:37
  246.0 3.0 %collective-permute-start.44 = (bf16[256,256]{1,0:T(8,128)(2,1)S(1)}, bf16[256,256]{1,0:T(8,128)(2,1)S(1)}, u32[]{:S(2)}, u32[]{:S(2)}) collective-permute-start(bf16[256,256]{1,0:T(8,128)(2,1)S(1)} %get-tuple-element.186), channel_id=1, source_target_pairs={{0,3},{1,2},{2,1},{3,0},{4,7},{5,6},{6,5},{7,4},{8,11},{9,10},{10,... | collective-permute-start | bytes 393224 | tf_op jit(solution)/shard_map/gco_z3/ppermute | solution.py:49
  250.4 6.6 %collective-permute-done.43.refs_2_ = bf16[256,256]{1,0:T(8,128)(2,1)S(1)} collective-permute-done((bf16[256,256]{1,0:T(8,128)(2,1)S(1)}, bf16[256,256]{1,0:T(8,128)(2,1)S(1)}, u32[]{:S(2)}, u32[]{:S(2)}) %collective-permute-start.43) | collective-permute-done | bytes 131104 | tf_op jit(solution)/shard_map/gco_z2/ppermute | solution.py:49
  257.0 1.7 collective-permute-start.41
  258.7 1.1 add_convert_fusion.13
  260.6 5.2 %collective-permute-done.40.refs_2_ = bf16[336,256]{1,0:T(8,128)(2,1)S(1)} collective-permute-done((bf16[336,256]{1,0:T(8,128)(2,1)S(1)}, bf16[336,256]{1,0:T(8,128)(2,1)S(1)}, u32[]{:S(2)}, u32[]{:S(2)}) %collective-permute-start.40) | collective-permute-done | bytes 172064 | tf_op jit(solution)/shard_map/gbu_z2/ppermute | solution.py:49
  265.8 1.2 finish_bu.1
  268.7 1.1 copy.62
  269.8 1.9 copy.61
  (148 shorter events, 24.9 us)
Async XLA Ops:
  0.6 2.4 copy-start.14
  0.7 2.6 copy-start.12
  4.1 10.4 %copy-start.15 = (s32[16]{0:T(128)S(1)}, s32[16]{0:T(128)}, u32[]{:S(2)}) copy-start(s32[16]{0:T(128)} %param.14) | copy-start | bytes 196
  4.1 10.7 %copy-start.16 = (s32[64]{0:T(128)S(1)}, s32[64]{0:T(128)}, u32[]{:S(2)}) copy-start(s32[64]{0:T(128)} %param.16) | copy-start | bytes 772
  4.1 10.8 %copy-start.20 = (s32[16]{0:T(128)S(1)}, s32[16]{0:T(128)}, u32[]{:S(2)}) copy-start(s32[16]{0:T(128)} %param.15) | copy-start | bytes 196
  4.2 17.0 %copy-start.13 = (bf16[8,32,1024]{2,1,0:T(8,128)(2,1)S(1)}, bf16[8,32,1024]{2,1,0:T(8,128)(2,1)}, u32[]{:S(2)}) copy-start(bf16[8,32,1024]{2,1,0:T(8,128)(2,1)} %param.13) | copy-start | bytes 1572868
  4.2 17.9 %copy-start.17 = (bf16[3,128]{1,0:T(4,128)(2,1)S(1)}, bf16[3,128]{1,0:T(4,128)(2,1)}, u32[]{:S(2)}) copy-start(bf16[3,128]{1,0:T(4,128)(2,1)} %param.19) | copy-start | bytes 2308
  4.3 17.9 %copy-start.18 = (bf16[128]{0:T(256)(128)(2,1)S(1)}, bf16[128]{0:T(256)(128)(2,1)}, u32[]{:S(2)}) copy-start(bf16[128]{0:T(256)(128)(2,1)} %param.21) | copy-start | bytes 772
  4.3 17.9 %copy-start.19 = (bf16[128]{0:T(256)(128)(2,1)S(1)}, bf16[128]{0:T(256)(128)(2,1)}, u32[]{:S(2)}) copy-start(bf16[128]{0:T(256)(128)(2,1)} %param.17) | copy-start | bytes 772
  4.3 26.6 %copy-start = (bf16[128,3456]{1,0:T(8,128)(2,1)}, bf16[128,3456]{1,0:T(8,128)(2,1)S(1)}, u32[]{:S(2)}) copy-start(bf16[128,3456]{1,0:T(8,128)(2,1)S(1)} %pad_maximum_fusion.1.refs_0_) | copy-start | bytes 2654212
  4.4 16.2 %collective-permute-start.2 = (bf16[512,256]{1,0:T(8,128)(2,1)S(1)}, bf16[512,256]{1,0:T(8,128)(2,1)S(1)}, u32[]{:S(2)}, u32[]{:S(2)}) collective-permute-start(bf16[512,256]{1,0:T(8,128)(2,1)S(1)} %bitcast.84), channel_id=1, source_target_pairs={{0,2},{1,3},{2,0},{3,1},{4,6},{5,7},{6,4},{7,5},{8,10},{9,11},{10,... | collective-permute-start | bytes 786440 | tf_op jit(solution)/shard_map/mix_z2/ppermute | solution.py:49
  8.5 13.7 %collective-permute-start.1 = (bf16[512,256]{1,0:T(8,128)(2,1)S(1)}, bf16[512,256]{1,0:T(8,128)(2,1)S(1)}, u32[]{:S(2)}, u32[]{:S(2)}) collective-permute-start(bf16[512,256]{1,0:T(8,128)(2,1)S(1)} %bitcast.85), channel_id=1, source_target_pairs={{0,1},{1,0},{2,3},{3,2},{4,5},{5,4},{6,7},{7,6},{8,9},{9,8},{10,11... | collective-permute-start | bytes 786440 | tf_op jit(solution)/shard_map/mix_z1/ppermute | solution.py:49
  10.1 20.8 %collective-permute-start.5 = (bf16[128,3456]{1,0:T(8,128)(2,1)S(1)}, bf16[128,3456]{1,0:T(8,128)(2,1)S(1)}, u32[]{:S(2)}, u32[]{:S(2)}) collective-permute-start(bf16[128,3456]{1,0:T(8,128)(2,1)S(1)} %pad_maximum_fusion.1.refs_0_), channel_id=1, source_target_pairs={{0,16},{4,20},{8,24},{12,28},{16,0},{20,4},{24,8},{28,12},{1,17},{... | collective-permute-start | bytes 2654216 | tf_op jit(solution)/shard_map/ffn_dp4/ppermute | solution.py:37
  11.6 20.7 %collective-permute-start.4 = (bf16[128,3456]{1,0:T(8,128)(2,1)S(1)}, bf16[128,3456]{1,0:T(8,128)(2,1)}, u32[]{:S(2)}, u32[]{:S(2)}) collective-permute-start(bf16[128,3456]{1,0:T(8,128)(2,1)S(1)} %pad_maximum_fusion.1.refs_0_), channel_id=1, source_target_pairs={{0,8},{4,12},{8,0},{12,4},{16,24},{20,28},{24,16},{28,20},{1,9},{5... | collective-permute-start | bytes 2654216 | tf_op jit(solution)/shard_map/ffn_dp2/ppermute | solution.py:37
  14.0 8.2 %collective-permute-start = (bf16[16,1024]{1,0:T(8,128)(2,1)S(1)}, bf16[16,1024]{1,0:T(8,128)(2,1)S(1)}, u32[]{:S(2)}, u32[]{:S(2)}) collective-permute-start(bf16[16,1024]{1,0:T(8,128)(2,1)S(1)} %reshape.217), channel_id=1, source_target_pairs={{0,1},{1,2},{2,3},{3,0},{4,5},{5,6},{6,7},{7,4},{8,9},{9,10},{10,1... | collective-permute-start | bytes 98312 | tf_op jit(solution)/shard_map/tail_z/ppermute | solution.py:43
  20.5 7.4 %collective-permute-start.3 = (bf16[512,256]{1,0:T(8,128)(2,1)S(1)}, bf16[512,256]{1,0:T(8,128)(2,1)S(1)}, u32[]{:S(2)}, u32[]{:S(2)}) collective-permute-start(bf16[512,256]{1,0:T(8,128)(2,1)S(1)} %collective-permute-done.2.refs_2_), channel_id=1, source_target_pairs={{0,1},{1,0},{2,3},{3,2},{4,5},{5,4},{6,7},{7,6},{8,9},{9,8},{10,11... | collective-permute-start | bytes 786440 | tf_op jit(solution)/shard_map/mix_on_z1/ppermute | solution.py:49
  32.2 24.7 %collective-permute-start.9 = (bf16[544,1024]{1,0:T(8,128)(2,1)S(1)}, bf16[544,1024]{1,0:T(8,128)(2,1)S(1)}, u32[]{:S(2)}, u32[]{:S(2)}) collective-permute-start(bf16[544,1024]{1,0:T(8,128)(2,1)S(1)} %stack_mixer.1.refs_0_), channel_id=1, source_target_pairs={{0,16},{4,20},{8,24},{12,28},{16,0},{20,4},{24,8},{28,12},{1,17},{... | collective-permute-start | bytes 3342344 | tf_op jit(solution)/shard_map/mix_dp4/ppermute | solution.py:37
  33.4 24.7 %collective-permute-start.7 = (bf16[544,1024]{1,0:T(8,128)(2,1)S(1)}, bf16[544,1024]{1,0:T(8,128)(2,1)S(1)}, u32[]{:S(2)}, u32[]{:S(2)}) collective-permute-start(bf16[544,1024]{1,0:T(8,128)(2,1)S(1)} %stack_mixer.1.refs_0_), channel_id=1, source_target_pairs={{0,8},{4,12},{8,0},{12,4},{16,24},{20,28},{24,16},{28,20},{1,9},{5... | collective-permute-start | bytes 3342344 | tf_op jit(solution)/shard_map/mix_dp2/ppermute | solution.py:37
  34.9 23.3 %collective-permute-start.13 = (bf16[128,3456]{1,0:T(8,128)(2,1)}, bf16[128,3456]{1,0:T(8,128)(2,1)}, u32[]{:S(2)}, u32[]{:S(2)}) collective-permute-start(bf16[128,3456]{1,0:T(8,128)(2,1)} %copy-done), channel_id=1, source_target_pairs={{0,4},{4,0},{8,12},{12,8},{16,20},{20,16},{24,28},{28,24},{1,5},{5... | collective-permute-start | bytes 2654216 | tf_op jit(solution)/shard_map/ffn_dp1/ppermute | solution.py:37
  34.9 25.6 %collective-permute-start.12 = (bf16[256,1024]{1,0:T(8,128)(2,1)}, bf16[256,1024]{1,0:T(8,128)(2,1)}, u32[]{:S(2)}, u32[]{:S(2)}) collective-permute-start(bf16[256,1024]{1,0:T(8,128)(2,1)} %bitcast.7.d_ref.refs_4_), channel_id=1, source_target_pairs={{0,1},{1,0},{2,3},{3,2},{4,5},{5,4},{6,7},{7,6},{8,9},{9,8},{10,11... | collective-permute-start | bytes 1572872 | tf_op jit(solution)/shard_map/dy_z1/ppermute | solution.py:49
  35.4 27.0 %collective-permute-start.11 = (bf16[256,1024]{1,0:T(8,128)(2,1)}, bf16[256,1024]{1,0:T(8,128)(2,1)}, u32[]{:S(2)}, u32[]{:S(2)}) collective-permute-start(bf16[256,1024]{1,0:T(8,128)(2,1)} %bitcast.7.d_ref.refs_4_), channel_id=1, source_target_pairs={{0,2},{1,3},{2,0},{3,1},{4,6},{5,7},{6,4},{7,5},{8,10},{9,11},{10,... | collective-permute-start | bytes 1572872 | tf_op jit(solution)/shard_map/dy_z2/ppermute | solution.py:49
  38.4 41.2 %copy-start.3 = (bf16[128,3456]{1,0:T(8,128)(2,1)S(1)}, bf16[128,3456]{1,0:T(8,128)(2,1)}, u32[]{:S(2)}) copy-start(bf16[128,3456]{1,0:T(8,128)(2,1)} %copy-done.2) | copy-start | bytes 2654212
  62.4 16.8 %collective-permute-start.14 = (bf16[544,1024]{1,0:T(8,128)(2,1)S(1)}, bf16[544,1024]{1,0:T(8,128)(2,1)}, u32[]{:S(2)}, u32[]{:S(2)}) collective-permute-start(bf16[544,1024]{1,0:T(8,128)(2,1)S(1)} %broadcast_select_fusion), channel_id=1, source_target_pairs={{0,16},{4,12},{8,24},{12,4},{16,0},{20,28},{24,8},{28,20},{1,17},{... | collective-permute-start | bytes 3342344 | tf_op jit(solution)/shard_map/mix_corner/ppermute | solution.py:97
  62.9 15.3 %collective-permute-start.15 = (bf16[128,3456]{1,0:T(8,128)(2,1)}, bf16[128,3456]{1,0:T(8,128)(2,1)S(1)}, u32[]{:S(2)}, u32[]{:S(2)}) collective-permute-start(bf16[128,3456]{1,0:T(8,128)(2,1)} %collective-permute-done.4.refs_2_), channel_id=1, source_target_pairs={{0,4},{4,0},{8,12},{12,8},{16,20},{20,16},{24,28},{28,24},{1,5},{5... | collective-permute-start | bytes 2654216 | tf_op jit(solution)/shard_map/ffn_dp1/ppermute | solution.py:37
  62.9 14.5 %collective-permute-start.16 = (bf16[256,1024]{1,0:T(8,128)(2,1)}, bf16[256,1024]{1,0:T(8,128)(2,1)S(1)}, u32[]{:S(2)}, u32[]{:S(2)}) collective-permute-start(bf16[256,1024]{1,0:T(8,128)(2,1)} %collective-permute-done.11.d_ref), channel_id=1, source_target_pairs={{0,1},{1,0},{2,3},{3,2},{4,5},{5,4},{6,7},{7,6},{8,9},{9,8},{10,11... | collective-permute-start | bytes 1572872 | tf_op jit(solution)/shard_map/dy_on_z1/ppermute | solution.py:49
  63.2 21.3 %collective-permute-start.6 = (bf16[544,1024]{1,0:T(8,128)(2,1)S(1)}, bf16[544,1024]{1,0:T(8,128)(2,1)}, u32[]{:S(2)}, u32[]{:S(2)}) collective-permute-start(bf16[544,1024]{1,0:T(8,128)(2,1)S(1)} %stack_mixer.1.refs_0_), channel_id=1, source_target_pairs={{0,4},{4,0},{8,12},{12,8},{16,20},{20,16},{24,28},{28,24},{1,5},{5... | collective-permute-start | bytes 3342344 | tf_op jit(solution)/shard_map/mix_dp1/ppermute | solution.py:37
  63.4 21.2 %collective-permute-start.10 = (bf16[544,1024]{1,0:T(8,128)(2,1)S(1)}, bf16[544,1024]{1,0:T(8,128)(2,1)}, u32[]{:S(2)}, u32[]{:S(2)}) collective-permute-start(bf16[544,1024]{1,0:T(8,128)(2,1)S(1)} %collective-permute-done.9.refs_4_), channel_id=1, source_target_pairs={{0,4},{4,0},{8,12},{12,8},{16,20},{20,16},{24,28},{28,24},{1,5},{5... | collective-permute-start | bytes 3342344 | tf_op jit(solution)/shard_map/mix_dp1/ppermute | solution.py:37
  78.2 6.4 %collective-permute-start.8 = (bf16[544,1024]{1,0:T(8,128)(2,1)S(1)}, bf16[544,1024]{1,0:T(8,128)(2,1)}, u32[]{:S(2)}, u32[]{:S(2)}) collective-permute-start(bf16[544,1024]{1,0:T(8,128)(2,1)S(1)} %collective-permute-done.7.refs_2_), channel_id=1, source_target_pairs={{0,4},{4,0},{8,12},{12,8},{16,20},{20,16},{24,28},{28,24},{1,5},{5... | collective-permute-start | bytes 3342344 | tf_op jit(solution)/shard_map/mix_dp1/ppermute | solution.py:37
  79.2 5.5 %collective-permute-start.17 = (bf16[544,1024]{1,0:T(8,128)(2,1)}, bf16[544,1024]{1,0:T(8,128)(2,1)}, u32[]{:S(2)}, u32[]{:S(2)}) collective-permute-start(bf16[544,1024]{1,0:T(8,128)(2,1)} %collective-permute-done.14.refs_6_), channel_id=1, source_target_pairs={{0,4},{4,0},{8,12},{12,8},{16,20},{20,16},{24,28},{28,24},{1,5},{5... | collective-permute-start | bytes 3342344 | tf_op jit(solution)/shard_map/mix_dp1/ppermute | solution.py:37
  81.9 13.4 %collective-permute-start.19 = (bf16[128,3456]{1,0:T(8,128)(2,1)}, bf16[128,3456]{1,0:T(8,128)(2,1)}, u32[]{:S(2)}, u32[]{:S(2)}) collective-permute-start(bf16[128,3456]{1,0:T(8,128)(2,1)} %broadcast_select_fusion.1), channel_id=1, source_target_pairs={{0,16},{4,12},{8,24},{12,4},{16,0},{20,28},{24,8},{28,20},{1,17},{... | collective-permute-start | bytes 2654216 | tf_op jit(solution)/shard_map/ffn_corner/ppermute | solution.py:97
  84.5 4.0 %copy-start.5 = (bf16[8,32,1024]{2,1,0:T(8,128)(2,1)S(1)}, bf16[8,32,1024]{2,1,0:T(8,128)(2,1)}, u32[]{:S(2)}) copy-start(bf16[8,32,1024]{2,1,0:T(8,128)(2,1)} %param.12) | copy-start | bytes 1572868
  84.5 13.6 %collective-permute-start.18 = (bf16[128,3456]{1,0:T(8,128)(2,1)}, bf16[128,3456]{1,0:T(8,128)(2,1)S(1)}, u32[]{:S(2)}, u32[]{:S(2)}) collective-permute-start(bf16[128,3456]{1,0:T(8,128)(2,1)} %copy-done.2), channel_id=1, source_target_pairs={{0,4},{4,0},{8,12},{12,8},{16,20},{20,16},{24,28},{28,24},{1,5},{5... | collective-permute-start | bytes 2654216 | tf_op jit(solution)/shard_map/ffn_dp1/ppermute | solution.py:37
  91.0 7.1 %copy-start.1 = (bf16[128,3456]{1,0:T(8,128)(2,1)S(1)}, bf16[128,3456]{1,0:T(8,128)(2,1)}, u32[]{:S(2)}) copy-start(bf16[128,3456]{1,0:T(8,128)(2,1)} %copy-done) | copy-start | bytes 2654212
  91.0 7.1 %copy-start.4 = (bf16[128,3456]{1,0:T(8,128)(2,1)S(1)}, bf16[128,3456]{1,0:T(8,128)(2,1)}, u32[]{:S(2)}) copy-start(bf16[128,3456]{1,0:T(8,128)(2,1)} %copy-done.2) | copy-start | bytes 2654212
  91.0 7.1 %copy-start.7 = (bf16[128,3456]{1,0:T(8,128)(2,1)S(1)}, bf16[128,3456]{1,0:T(8,128)(2,1)}, u32[]{:S(2)}) copy-start(bf16[128,3456]{1,0:T(8,128)(2,1)} %copy-done.6) | copy-start | bytes 2654212
  95.2 2.9 %collective-permute-start.20 = (bf16[128,3456]{1,0:T(8,128)(2,1)}, bf16[128,3456]{1,0:T(8,128)(2,1)S(1)}, u32[]{:S(2)}, u32[]{:S(2)}) collective-permute-start(bf16[128,3456]{1,0:T(8,128)(2,1)} %collective-permute-done.19.refs_6_), channel_id=1, source_target_pairs={{0,4},{4,0},{8,12},{12,8},{16,20},{20,16},{24,28},{28,24},{1,5},{5... | collective-permute-start | bytes 2654216 | tf_op jit(solution)/shard_map/ffn_dp1/ppermute | solution.py:37
  95.2 26.3 %collective-permute-start.22 = (bf16[256,1024]{1,0:T(8,128)(2,1)S(1)}, bf16[256,1024]{1,0:T(8,128)(2,1)S(1)}, u32[]{:S(2)}, u32[]{:S(2)}) collective-permute-start(bf16[256,1024]{1,0:T(8,128)(2,1)S(1)} %get-tuple-element.118.n_ref), channel_id=1, source_target_pairs={{0,2},{1,3},{2,0},{3,1},{4,6},{5,7},{6,4},{7,5},{8,10},{9,11},{10,... | collective-permute-start | bytes 1572872 | tf_op jit(solution)/shard_map/n2_z2/ppermute | solution.py:49
  96.4 25.3 %collective-permute-start.21 = (bf16[256,1024]{1,0:T(8,128)(2,1)S(1)}, bf16[256,1024]{1,0:T(8,128)(2,1)S(1)}, u32[]{:S(2)}, u32[]{:S(2)}) collective-permute-start(bf16[256,1024]{1,0:T(8,128)(2,1)S(1)} %get-tuple-element.118.n_ref), channel_id=1, source_target_pairs={{0,1},{1,0},{2,3},{3,2},{4,5},{5,4},{6,7},{7,6},{8,9},{9,8},{10,11... | collective-permute-start | bytes 1572872 | tf_op jit(solution)/shard_map/n2_z1/ppermute | solution.py:49
  121.5 13.8 %collective-permute-start.23 = (bf16[256,1024]{1,0:T(8,128)(2,1)S(1)}, bf16[256,1024]{1,0:T(8,128)(2,1)S(1)}, u32[]{:S(2)}, u32[]{:S(2)}) collective-permute-start(bf16[256,1024]{1,0:T(8,128)(2,1)S(1)} %collective-permute-done.22.n_ref), channel_id=1, source_target_pairs={{0,1},{1,0},{2,3},{3,2},{4,5},{5,4},{6,7},{7,6},{8,9},{9,8},{10,11... | collective-permute-start | bytes 1572872 | tf_op jit(solution)/shard_map/n2_on_z1/ppermute | solution.py:49
  128.8 6.6 %copy-start.9 = (bf16[256,1024]{1,0:T(8,128)(2,1)S(1)}, bf16[256,1024]{1,0:T(8,128)(2,1)}, u32[]{:S(2)}) copy-start(bf16[256,1024]{1,0:T(8,128)(2,1)} %copy-done.8) | copy-start | bytes 1572868
  139.7 14.9 %collective-permute-start.29 = (bf16[256,1024]{1,0:T(8,128)(2,1)S(1)}, bf16[256,1024]{1,0:T(8,128)(2,1)S(1)}, u32[]{:S(2)}, u32[]{:S(2)}) collective-permute-start(bf16[256,1024]{1,0:T(8,128)(2,1)S(1)} %get-tuple-element.151), channel_id=1, source_target_pairs={{0,1},{1,0},{2,3},{3,2},{4,5},{5,4},{6,7},{7,6},{8,9},{9,8},{10,11... | collective-permute-start | bytes 1572872 | tf_op jit(solution)/shard_map/dn_on_z1/ppermute | solution.py:49
  140.6 34.1 %collective-permute-start.24 = (bf16[256,1024]{1,0:T(8,128)(2,1)S(1)}, bf16[256,1024]{1,0:T(8,128)(2,1)S(1)}, u32[]{:S(2)}, u32[]{:S(2)}) collective-permute-start(bf16[256,1024]{1,0:T(8,128)(2,1)S(1)} %get-tuple-element.131), channel_id=1, source_target_pairs={{0,1},{1,0},{2,3},{3,2},{4,5},{5,4},{6,7},{7,6},{8,9},{9,8},{10,11... | collective-permute-start | bytes 1572872 | tf_op jit(solution)/shard_map/dn_z1/ppermute | solution.py:49
  154.8 22.2 %collective-permute-start.30 = (bf16[256,1024]{1,0:T(8,128)(2,1)S(1)}, bf16[256,1024]{1,0:T(8,128)(2,1)S(1)}, u32[]{:S(2)}, u32[]{:S(2)}) collective-permute-start(bf16[256,1024]{1,0:T(8,128)(2,1)S(1)} %add_convert_fusion.12), channel_id=1, source_target_pairs={{0,2},{1,3},{2,0},{3,1},{4,6},{5,7},{6,4},{7,5},{8,10},{9,11},{10,... | collective-permute-start | bytes 1572872 | tf_op jit(solution)/shard_map/dn_z2/ppermute | solution.py:49
  156.4 27.6 %collective-permute-start.28 = (bf16[4,128,3456]{2,1,0:T(8,128)(2,1)S(1)}, bf16[4,128,3456]{2,1,0:T(8,128)(2,1)S(1)}, u32[]{:S(2)}, u32[]{:S(2)}) collective-permute-start(bf16[4,128,3456]{2,1,0:T(8,128)(2,1)S(1)} %get-tuple-element.149), channel_id=1, source_target_pairs={{0,4},{4,0},{8,12},{12,8},{16,20},{20,16},{24,28},{28,24},{1,5},{5... | collective-permute-start | bytes 10616840 | tf_op jit(solution)/shard_map/gf_dp1/ppermute | solution.py:37
  174.7 12.7 %collective-permute-start.26 = (bf16[256,1024]{1,0:T(8,128)(2,1)S(1)}, bf16[256,1024]{1,0:T(8,128)(2,1)S(1)}, u32[]{:S(2)}, u32[]{:S(2)}) collective-permute-start(bf16[256,1024]{1,0:T(8,128)(2,1)S(1)} %get-tuple-element.143), channel_id=1, source_target_pairs={{0,1},{1,0},{2,3},{3,2},{4,5},{5,4},{6,7},{7,6},{8,9},{9,8},{10,11... | collective-permute-start | bytes 1572872 | tf_op jit(solution)/shard_map/out_on_z1/ppermute | solution.py:49
  187.4 4.4 %collective-permute-start.32 = (bf16[4,256,1024]{2,1,0:T(8,128)(2,1)S(1)}, bf16[4,256,1024]{2,1,0:T(8,128)(2,1)S(1)}, u32[]{:S(2)}, u32[]{:S(2)}) collective-permute-start(bf16[4,256,1024]{2,1,0:T(8,128)(2,1)S(1)} %get-tuple-element.176), channel_id=1, source_target_pairs={{0,4},{4,0},{8,12},{12,8},{16,20},{20,16},{24,28},{28,24},{1,5},{5... | collective-permute-start | bytes 6291464 | tf_op jit(solution)/shard_map/gco_dp1/ppermute | solution.py:37
  191.2 4.7 %collective-permute-start.31 = (bf16[4,288,1024]{2,1,0:T(8,128)(2,1)S(1)}, bf16[4,288,1024]{2,1,0:T(8,128)(2,1)S(1)}, u32[]{:S(2)}, u32[]{:S(2)}) collective-permute-start(bf16[4,288,1024]{2,1,0:T(8,128)(2,1)S(1)} %get-tuple-element.174), channel_id=1, source_target_pairs={{0,4},{4,0},{8,12},{12,8},{16,20},{20,16},{24,28},{28,24},{1,5},{5... | collective-permute-start | bytes 7077896 | tf_op jit(solution)/shard_map/gbu_dp1/ppermute | solution.py:37
  192.2 9.5 %collective-permute-start.33 = (bf16[256,1024]{1,0:T(8,128)(2,1)S(1)}, bf16[256,1024]{1,0:T(8,128)(2,1)S(1)}, u32[]{:S(2)}, u32[]{:S(2)}) collective-permute-start(bf16[256,1024]{1,0:T(8,128)(2,1)S(1)} %get-tuple-element.232), channel_id=1, source_target_pairs={{0,16},{4,12},{8,24},{12,4},{16,0},{20,28},{24,8},{28,20},{1,17},{... | collective-permute-start | bytes 1572872 | tf_op jit(solution)/shard_map/gco_corner/ppermute | solution.py:97
  196.4 14.9 %collective-permute-start.36 = (bf16[288,1024]{1,0:T(8,128)(2,1)S(1)}, bf16[288,1024]{1,0:T(8,128)(2,1)S(1)}, u32[]{:S(2)}, u32[]{:S(2)}) collective-permute-start(bf16[288,1024]{1,0:T(8,128)(2,1)S(1)} %get-tuple-element.228), channel_id=1, source_target_pairs={{0,16},{4,12},{8,24},{12,4},{16,0},{20,28},{24,8},{28,20},{1,17},{... | collective-permute-start | bytes 1769480 | tf_op jit(solution)/shard_map/gbu_corner/ppermute | solution.py:97
  198.0 28.9 %collective-permute-start.45 = (bf16[128,3456]{1,0:T(8,128)(2,1)S(1)}, bf16[128,3456]{1,0:T(8,128)(2,1)S(1)}, u32[]{:S(2)}, u32[]{:S(2)}) collective-permute-start(bf16[128,3456]{1,0:T(8,128)(2,1)S(1)} %fusion.13), channel_id=1, source_target_pairs={{0,16},{4,12},{8,24},{12,4},{16,0},{20,28},{24,8},{28,20},{1,17},{... | collective-permute-start | bytes 2654216 | tf_op jit(solution)/shard_map/gf_corner/ppermute | solution.py:97
  198.5 37.7 %collective-permute-start.25 = (bf16[256,1024]{1,0:T(8,128)(2,1)S(1)}, bf16[256,1024]{1,0:T(8,128)(2,1)S(1)}, u32[]{:S(2)}, u32[]{:S(2)}) collective-permute-start(bf16[256,1024]{1,0:T(8,128)(2,1)S(1)} %get-tuple-element.132), channel_id=1, source_target_pairs={{0,1},{1,0},{2,3},{3,2},{4,5},{5,4},{6,7},{7,6},{8,9},{9,8},{10,11... | collective-permute-start | bytes 1572872 | tf_op jit(solution)/shard_map/out_z1/ppermute | solution.py:49
  199.7 25.6 %collective-permute-start.27 = (bf16[256,1024]{1,0:T(8,128)(2,1)S(1)}, bf16[256,1024]{1,0:T(8,128)(2,1)S(1)}, u32[]{:S(2)}, u32[]{:S(2)}) collective-permute-start(bf16[256,1024]{1,0:T(8,128)(2,1)S(1)} %add_convert_fusion.14), channel_id=1, source_target_pairs={{0,2},{1,3},{2,0},{3,1},{4,6},{5,7},{6,4},{7,5},{8,10},{9,11},{10,... | collective-permute-start | bytes 1572872 | tf_op jit(solution)/shard_map/out_z2/ppermute | solution.py:49
  202.2 31.1 %collective-permute-start.35 = (bf16[256,1024]{1,0:T(8,128)(2,1)S(1)}, bf16[256,1024]{1,0:T(8,128)(2,1)S(1)}, u32[]{:S(2)}, u32[]{:S(2)}) collective-permute-start(bf16[256,1024]{1,0:T(8,128)(2,1)S(1)} %get-tuple-element.230), channel_id=1, source_target_pairs={{0,16},{4,20},{8,24},{12,28},{16,0},{20,4},{24,8},{28,12},{1,17},{... | collective-permute-start | bytes 1572872 | tf_op jit(solution)/shard_map/gco_dp4/ppermute | solution.py:37
  211.3 22.6 %collective-permute-start.34 = (bf16[256,1024]{1,0:T(8,128)(2,1)S(1)}, bf16[256,1024]{1,0:T(8,128)(2,1)S(1)}, u32[]{:S(2)}, u32[]{:S(2)}) collective-permute-start(bf16[256,1024]{1,0:T(8,128)(2,1)S(1)} %get-tuple-element.231), channel_id=1, source_target_pairs={{0,8},{4,12},{8,0},{12,4},{16,24},{20,28},{24,16},{28,20},{1,9},{5... | collective-permute-start | bytes 1572872 | tf_op jit(solution)/shard_map/gco_dp2/ppermute | solution.py:37
  225.3 20.7 %collective-permute-start.38 = (bf16[288,1024]{1,0:T(8,128)(2,1)S(1)}, bf16[288,1024]{1,0:T(8,128)(2,1)S(1)}, u32[]{:S(2)}, u32[]{:S(2)}) collective-permute-start(bf16[288,1024]{1,0:T(8,128)(2,1)S(1)} %get-tuple-element.226), channel_id=1, source_target_pairs={{0,16},{4,20},{8,24},{12,28},{16,0},{20,4},{24,8},{28,12},{1,17},{... | collective-permute-start | bytes 1769480 | tf_op jit(solution)/shard_map/gbu_dp4/ppermute | solution.py:37
  226.8 19.2 %collective-permute-start.37 = (bf16[288,1024]{1,0:T(8,128)(2,1)S(1)}, bf16[288,1024]{1,0:T(8,128)(2,1)S(1)}, u32[]{:S(2)}, u32[]{:S(2)}) collective-permute-start(bf16[288,1024]{1,0:T(8,128)(2,1)S(1)} %get-tuple-element.227), channel_id=1, source_target_pairs={{0,8},{4,12},{8,0},{12,4},{16,24},{20,28},{24,16},{28,20},{1,9},{5... | collective-permute-start | bytes 1769480 | tf_op jit(solution)/shard_map/gbu_dp2/ppermute | solution.py:37
  233.4 34.7 %collective-permute-start.46 = (bf16[128,3456]{1,0:T(8,128)(2,1)S(1)}, bf16[128,3456]{1,0:T(8,128)(2,1)S(1)}, u32[]{:S(2)}, u32[]{:S(2)}) collective-permute-start(bf16[128,3456]{1,0:T(8,128)(2,1)S(1)} %get-tuple-element.193), channel_id=1, source_target_pairs={{0,8},{4,12},{8,0},{12,4},{16,24},{20,28},{24,16},{28,20},{1,9},{5... | collective-permute-start | bytes 2654216 | tf_op jit(solution)/shard_map/gf_dp2/ppermute | solution.py:37
  233.9 34.2 %collective-permute-start.47 = (bf16[128,3456]{1,0:T(8,128)(2,1)S(1)}, bf16[128,3456]{1,0:T(8,128)(2,1)S(1)}, u32[]{:S(2)}, u32[]{:S(2)}) collective-permute-start(bf16[128,3456]{1,0:T(8,128)(2,1)S(1)} %get-tuple-element.194), channel_id=1, source_target_pairs={{0,16},{4,20},{8,24},{12,28},{16,0},{20,4},{24,8},{28,12},{1,17},{... | collective-permute-start | bytes 2654216 | tf_op jit(solution)/shard_map/gf_dp4/ppermute | solution.py:37
  236.2 13.6 %collective-permute-start.42 = (bf16[256,256]{1,0:T(8,128)(2,1)S(1)}, bf16[256,256]{1,0:T(8,128)(2,1)S(1)}, u32[]{:S(2)}, u32[]{:S(2)}) collective-permute-start(bf16[256,256]{1,0:T(8,128)(2,1)S(1)} %get-tuple-element.184), channel_id=1, source_target_pairs={{0,1},{1,0},{2,3},{3,2},{4,5},{5,4},{6,7},{7,6},{8,9},{9,8},{10,11... | collective-permute-start | bytes 393224 | tf_op jit(solution)/shard_map/gco_z1/ppermute | solution.py:49
  246.0 11.0 %collective-permute-start.43 = (bf16[256,256]{1,0:T(8,128)(2,1)S(1)}, bf16[256,256]{1,0:T(8,128)(2,1)S(1)}, u32[]{:S(2)}, u32[]{:S(2)}) collective-permute-start(bf16[256,256]{1,0:T(8,128)(2,1)S(1)} %get-tuple-element.185), channel_id=1, source_target_pairs={{0,2},{1,3},{2,0},{3,1},{4,6},{5,7},{6,4},{7,5},{8,10},{9,11},{10,... | collective-permute-start | bytes 393224 | tf_op jit(solution)/shard_map/gco_z2/ppermute | solution.py:49
  246.0 11.0 %collective-permute-start.44 = (bf16[256,256]{1,0:T(8,128)(2,1)S(1)}, bf16[256,256]{1,0:T(8,128)(2,1)S(1)}, u32[]{:S(2)}, u32[]{:S(2)}) collective-permute-start(bf16[256,256]{1,0:T(8,128)(2,1)S(1)} %get-tuple-element.186), channel_id=1, source_target_pairs={{0,3},{1,2},{2,1},{3,0},{4,7},{5,6},{6,5},{7,4},{8,11},{9,10},{10,... | collective-permute-start | bytes 393224 | tf_op jit(solution)/shard_map/gco_z3/ppermute | solution.py:49
  249.8 10.8 %collective-permute-start.39 = (bf16[336,256]{1,0:T(8,128)(2,1)S(1)}, bf16[336,256]{1,0:T(8,128)(2,1)S(1)}, u32[]{:S(2)}, u32[]{:S(2)}) collective-permute-start(bf16[336,256]{1,0:T(8,128)(2,1)S(1)} %get-tuple-element.181), channel_id=1, source_target_pairs={{0,1},{1,0},{2,3},{3,2},{4,5},{5,4},{6,7},{7,6},{8,9},{9,8},{10,11... | collective-permute-start | bytes 516104 | tf_op jit(solution)/shard_map/gbu_z1/ppermute | solution.py:49
  257.0 8.8 %collective-permute-start.40 = (bf16[336,256]{1,0:T(8,128)(2,1)S(1)}, bf16[336,256]{1,0:T(8,128)(2,1)S(1)}, u32[]{:S(2)}, u32[]{:S(2)}) collective-permute-start(bf16[336,256]{1,0:T(8,128)(2,1)S(1)} %get-tuple-element.182), channel_id=1, source_target_pairs={{0,2},{1,3},{2,0},{3,1},{4,6},{5,7},{6,4},{7,5},{8,10},{9,11},{10,... | collective-permute-start | bytes 516104 | tf_op jit(solution)/shard_map/gbu_z2/ppermute | solution.py:49
  257.0 8.7 %collective-permute-start.41 = (bf16[336,256]{1,0:T(8,128)(2,1)S(1)}, bf16[336,256]{1,0:T(8,128)(2,1)S(1)}, u32[]{:S(2)}, u32[]{:S(2)}) collective-permute-start(bf16[336,256]{1,0:T(8,128)(2,1)S(1)} %get-tuple-element.183), channel_id=1, source_target_pairs={{0,3},{1,2},{2,1},{3,0},{4,7},{5,6},{6,5},{7,4},{8,11},{9,10},{10,... | collective-permute-start | bytes 516104 | tf_op jit(solution)/shard_map/gbu_z3/ppermute | solution.py:49
  (5 other events, 4.4 us)
